TPU v7x, 512 devices: a whole 4x8x8 slice. The times are simulated.
512 devices in a mesh: ctx: 64 (over x, z, core), head: 8 (over y).
Axes of the slice: x: 4, y: 8, z: 8, core: 2. Of those that a mesh axis runs over, the one named last changes fastest.
Arguments:
- queries: bfloat16 [16384, 4096], P('ctx', 'head'), may hold values from -180 to 180
- keys: bfloat16 [16384, 1024], P('ctx', 'head'), may hold values from -6.5 to 6.5
- values: bfloat16 [16384, 1024], P('ctx', 'head'), may hold values from -6 to 6
- out_grad: bfloat16 [16384, 4096], P('ctx', 'head'), may hold values from -6 to 6
- attn_out: bfloat16 [16384, 4096], P('ctx', 'head'), may hold values from -6 to 6
- lengths: int32 [64], replicated, may hold values from 1 to 1792, as said below
- proj_weight: bfloat16 [4096, 8, 768], P('ctx', 'head'), may hold values from -0.078125 to 0.078125
Outputs:
- input_grad: bfloat16 [16384, 4096], P('ctx', 'head')
Inputs may be any that keep to these rules, and one draw needn't show every extreme that they name: `lengths`: every document has 1 to 1792 tokens, one has exactly 1792, and they sum to 16384.
All inputs are finite; a program needn't handle non-finite values.
Results may differ from a plain program's by a relative error of at most 0.013.
Values may be sent and summed in bfloat16 or wider, within the bound.
No kernel may reach another device: no remote copies, remote signals or barrier semaphores. Data moves between devices by JAX's collectives and lax.ppermute only.
A program may use at most 64 MiB of HBM per device.

v0:
```python
import jax
import jax.numpy as jnp
from jax import lax
from jax.experimental import pallas as pl
from jax.experimental.pallas import tpu as pltpu
from jax.sharding import PartitionSpec as P


HD = 128
GROUP = 4
TILE = 256
NX = 4
NZ = 8
NCHIP = NX * NZ
NHEAD = 8
SLOTS = 8
DOCS = 64
LOG2E = 1.4426950408889634
SCALE = HD ** (-0.5)
F32 = jnp.float32
BF16 = jnp.bfloat16


def ctx_of(x, z, c):
    return 2 * (NZ * (x % NX) + z % NZ) + c


def chip_shift(by):
    return [(2 * q + c, 2 * ((q + by) % NCHIP) + c) for q in range(NCHIP) for c in range(2)]


Z_RINGS = [[ctx_of(x, z, c) for z in range(NZ)] for x in range(NX) for c in range(2)]
X_SPLIT = [
    (ctx_of(x, z, c), ctx_of(x + 1 - 2 * c, z, c))
    for x in range(NX) for z in range(NZ) for c in range(2)
]
CORE_SWAP = [(d, d ^ 1) for d in range(2 * NCHIP)]
CORES = [[2 * q, 2 * q + 1] for q in range(NCHIP)]
LAST_TILE = [(2 * q, 2 * q + 1) for q in range(NCHIP)] + [
    (2 * q + 1, 2 * ((q + 4) % NCHIP)) for q in range(NCHIP)
]
LAST_TILE_BACK = [(b, a) for a, b in LAST_TILE]


WEIGHT_TRANSPOSE = [
    (ctx_of(x, z, c) * NHEAD + 2 * a + b, ctx_of(a, z, c) * NHEAD + 2 * x + b)
    for x in range(NX) for z in range(NZ) for c in range(2)
    for a in range(NX) for b in range(2)
]


def head_shift(by):
    return [(j, (j + by) % NHEAD) for j in range(NHEAD)]


SAME_PARITY = [[b + 2 * a for a in range(4)] for b in range(2)]
HEAD_PAIRS = [[2 * k, 2 * k + 1] for k in range(4)]

NT = (((1,), (1,)), ((), ()))
NN = (((1,), (0,)), ((), ()))
TN = (((0,), (0,)), ((), ()))


def dot(a, b, dims):
    return lax.dot_general(a, b, dims, preferred_element_type=F32)


def attention_kernel(
    me, lengths, q_ref, do_ref, out_ref, own, last, o1, o23, both,
    dq_ref, g_own, g_last, g_x, scores,
):
    i = me[0]
    chip, core = i // 2, i % 2
    other = 1 - core
    q_pos = i * TILE + lax.broadcasted_iota(jnp.int32, (1, TILE), 1)
    start = jnp.zeros((1, TILE), jnp.int32)
    end = jnp.int32(0)
    for d in range(DOCS):
        end = end + lengths[d]
        start = jnp.where(end <= q_pos, end, start)
    q_all = jnp.concatenate([q_ref[:, h * HD:(h + 1) * HD] for h in range(GROUP)], axis=0)
    do_all = jnp.concatenate([do_ref[:, h * HD:(h + 1) * HD] for h in range(GROUP)], axis=0)
    out_all = jnp.concatenate([out_ref[:, h * HD:(h + 1) * HD] for h in range(GROUP)], axis=0)
    prod = do_all.astype(F32) * out_all.astype(F32)
    high = prod.astype(BF16)
    low = (prod - high.astype(F32)).astype(BF16)
    ones = jnp.ones((16, HD), BF16)
    delta = (dot(ones, high, NT) + dot(ones, low, NT))[0:1, :]
    row = lax.broadcasted_iota(jnp.int32, (TILE, TILE), 0)
    last_tile = jnp.where(core == 1, 2 * chip, 2 * chip - 7)
    tiles = [
        (own, i), (o1, 2 * (chip - 1) + core), (o23.at[0], 2 * (chip - 2) + core),
        (o23.at[1], 2 * (chip - 3) + core), (last, last_tile),
    ] + [(both.at[other, n], 2 * (chip - 1 - n) + other) for n in range(3)]
    width = GROUP * TILE
    top = jnp.full((8, width), -1e30, F32)
    for t, (tile, number) in enumerate(tiles):
        raw = dot(tile[0], q_all, NT)
        k_pos = number * TILE + row
        allowed = (k_pos >= start) & (k_pos <= q_pos)
        parts = []
        for h in range(GROUP):
            part = jnp.where(allowed, raw[:, h * TILE:(h + 1) * TILE], -1e30)
            scores[pl.ds(t * TILE, TILE), pl.ds(h * TILE, TILE)] = part
            parts.append(jnp.max(part.reshape(TILE // 8, 8, TILE), axis=0))
        top = jnp.maximum(top, jnp.concatenate(parts, axis=1))
    top = jnp.max(top, axis=0, keepdims=True)
    total = jnp.zeros((8, width), F32)
    for t in range(SLOTS):
        e = jnp.exp2((scores[pl.ds(t * TILE, TILE), :] - top) * (SCALE * LOG2E))
        scores[pl.ds(t * TILE, TILE), :] = e
        total = total + jnp.sum(e.reshape(TILE // 8, 8, width), axis=0)
    total = jnp.sum(total, axis=0, keepdims=True)
    inv = 1.0 / total
    dq = [jnp.zeros((TILE, HD), F32) for _ in range(GROUP)]
    for t, (tile, _) in enumerate(tiles):
        probs = scores[pl.ds(t * TILE, TILE), :] * inv
        dprobs = dot(tile[1], do_all, NT)
        dscore = (probs * (dprobs - delta) * SCALE).astype(BF16)
        dv = dot(probs.astype(BF16), do_all, NN)
        dk = dot(dscore, q_all, NN)
        for h in range(GROUP):
            dq[h] = dq[h] + dot(dscore[:, h * TILE:(h + 1) * TILE], tile[0], TN)
        if t < 4:
            g_own[t, 0] = dk
            g_own[t, 1] = dv
        elif t == 4:
            g_last[0] = dk.astype(BF16)
            g_last[1] = dv.astype(BF16)
        else:
            g_x[t - 5, 0] = dk.astype(BF16)
            g_x[t - 5, 1] = dv.astype(BF16)
    for h in range(GROUP):
        dq_ref[:, h * HD:(h + 1) * HD] = dq[h].astype(BF16)


def project(me, heads, blocks, cols, acc_ref):
    x, core = me[1], me[3]
    up = 1 - 2 * core
    own, near, other, half, rest = blocks
    first, second = slice(0, 512), slice(512, 1024)
    here, behind, ahead = heads[x], heads[(x - up + NX) % NX], heads[(x + up + NX) % NX]
    far = heads[(x + 2) % NX]
    for side, rows, swapped, last in ((0, first, second, half), (1, second, first, rest)):
        acc_ref[side] = (
            acc_ref[side] + dot(here, own[rows, cols], NT) + dot(behind, near[rows, cols], NT)
            + dot(ahead, other[swapped, cols], NT) + dot(far, last[:, cols], NT)
        )


def proj_q_kernel(me, d0, d1, d2, d3, *refs):
    blocks, (acc_ref, heads) = refs[:5], refs[5:]
    for r, d in enumerate((d0, d1, d2, d3)):
        heads[(me[4] + r) % NX] = d[...]
    acc_ref[...] = jnp.zeros_like(acc_ref)
    project(me, heads, blocks, slice(0, 512), acc_ref)


def proj_kv_kernel(me, kv_ref, acc_in, *refs):
    blocks, (send_ref, keep_ref, heads, acc_ref, full) = refs[:5], refs[5:]
    core, b = me[3], me[5]
    for a in range(NX):
        heads[a, :, :HD] = kv_ref[a, 0]
        heads[a, :, HD:] = kv_ref[a, 1]
    acc_ref[...] = acc_in[...]
    project(me, heads, blocks, slice(512, 768), acc_ref)
    left = lax.broadcasted_iota(jnp.int32, (TILE, 128), 1) < 64
    for n in range(4):
        lanes = slice(128 * n, 128 * n + 128)
        even, odd = acc_ref[core, :, lanes], acc_ref[1 - core, :, lanes]
        at = (n % 2) * 256
        full[n // 2, :, at:at + 128] = jnp.where(left, even, pltpu.roll(odd, 64, 1))
        full[n // 2, :, at + 128:at + 256] = jnp.where(left, pltpu.roll(even, 64, 1), odd)
    send_ref[...] = full[1 - b].astype(BF16)
    keep_ref[...] = full[b]


def call(kernel, n_scalar, args, outs, scratch=(), flops=0, nbytes=0, mib=8):
    vmem = pl.BlockSpec(memory_space=pltpu.VMEM)
    smem = pl.BlockSpec(memory_space=pltpu.SMEM)
    return pl.pallas_call(
        kernel,
        out_shape=outs,
        in_specs=[smem] * n_scalar + [vmem] * (len(args) - n_scalar),
        out_specs=jax.tree.map(lambda _: vmem, outs),
        scratch_shapes=list(scratch),
        cost_estimate=pl.CostEstimate(flops=flops, bytes_accessed=nbytes, transcendentals=0),
        compiler_params=pltpu.CompilerParams(vmem_limit_bytes=mib * 1024 * 1024),
    )(*args)


def sds(shape, dtype):
    return jax.ShapeDtypeStruct(shape, dtype)


def gather(array, axis, groups):
    return lax.all_gather(array, axis, axis=0, axis_index_groups=groups)


def step(queries, keys, values, out_grad, attn_out, lengths, proj_weight):
    i = lax.axis_index("ctx")
    j = lax.axis_index("head")
    chip, core = i // 2, i % 2
    k, b = j // 2, j % 2
    me = jnp.stack([i, chip // NZ, chip % NZ, core, k, b]).astype(jnp.int32)

    own = jnp.stack([keys, values])
    o1 = lax.ppermute(own, "ctx", chip_shift(1))
    last = lax.ppermute(own, "ctx", LAST_TILE)
    o23 = lax.ppermute(jnp.stack([own, o1]), "ctx", chip_shift(2))
    both = gather(jnp.concatenate([o1[None], o23]), "ctx", CORES)

    w = lax.ppermute(proj_weight.reshape(64, 768), ("ctx", "head"), WEIGHT_TRANSPOSE)
    w = gather(w, "ctx", Z_RINGS).reshape(512, 768)
    w = jnp.concatenate([w, lax.ppermute(w, "ctx", CORE_SWAP)])
    w1 = lax.ppermute(w, "ctx", X_SPLIT)
    w2 = lax.ppermute(w1[:512], "ctx", X_SPLIT)
    weights = [w, w1, lax.ppermute(w1, "ctx", CORE_SWAP), w2, lax.ppermute(w2, "ctx", CORE_SWAP)]

    dq, g_own, g_last, g_x = call(
        attention_kernel, 2,
        [me, lengths, queries, out_grad, attn_out, own, last, o1, o23, both],
        (
            sds((TILE, GROUP * HD), BF16),
            sds((4, 2, TILE, HD), F32),
            sds((2, TILE, HD), BF16),
            sds((3, 2, TILE, HD), BF16),
        ),
        scratch=[pltpu.VMEM((SLOTS * TILE, GROUP * TILE), F32)],
        flops=2_700_000_000, nbytes=5_000_000, mib=18,
    )

    swapped = gather(g_x, "ctx", CORES)
    x_back = lax.dynamic_index_in_dim(swapped, 1 - core, 0, keepdims=False)
    far = (g_own[2:] + x_back[1:].astype(F32)).astype(BF16)
    far_back = lax.ppermute(far, "ctx", chip_shift(-2))
    last_back = lax.ppermute(g_last, "ctx", LAST_TILE_BACK)
    near = (g_own[1] + x_back[0].astype(F32) + far_back[1].astype(F32)).astype(BF16)
    near_back = lax.ppermute(near, "ctx", chip_shift(-1))
    kv = (
        g_own[0] + far_back[0].astype(F32) + near_back.astype(F32) + last_back.astype(F32)
    ).astype(BF16)

    dqs = [dq] + [lax.ppermute(dq, "head", head_shift(-2 * r)) for r in (1, 2, 3)]
    acc = call(
        proj_q_kernel, 1, [me] + dqs + weights, sds((2, TILE, 512), F32),
        scratch=[pltpu.VMEM((NX, TILE, 512), BF16)],
        flops=1_073_741_824, nbytes=6_000_000,
    )
    kvs = gather(kv, "head", SAME_PARITY)
    send, keep = call(
        proj_kv_kernel, 1, [me, kvs, acc] + weights,
        (sds((TILE, 512), BF16), sds((TILE, 512), F32)),
        scratch=[pltpu.VMEM((NX, TILE, 256), BF16)] + [pltpu.VMEM((2, TILE, 512), F32)] * 2,
        flops=536_870_912, nbytes=4_000_000,
    )
    got = gather(send, "head", HEAD_PAIRS)
    got = lax.dynamic_index_in_dim(got, 1 - b, 0, keepdims=False)
    return (keep + got.astype(F32)).astype(BF16)


def solution(mesh):
    placed = (
        P("ctx", "head"),
        P("ctx", "head"),
        P("ctx", "head"),
        P("ctx", "head"),
        P("ctx", "head"),
        P(),
        P("ctx", "head", None),
    )
    return jax.shard_map(
        step, mesh=mesh, in_specs=placed, out_specs=P("ctx", "head"), check_vma=False
    )
```

profile of v0, /device:TPU:6, one launch (start us, length us, event | category | flops | bytes accessed | tf_op | source)
XLA Modules:
  0.0 188.1 jit_solution(13085520507897592877)
XLA Ops:
  0.0 6.1 %collective-permute-start.9 = (bf16[64,768]{1,0:T(8,128)(2,1)}, bf16[64,768]{1,0:T(8,128)(2,1)S(1)}, u32[]{:S(2)}, u32[]{:S(2)}) collective-permute-start(bf16[64,768]{1,0:T(8,128)(2,1)} %bitcast.51), channel_id=1, source_target_pairs={{0,0},{1,1},{2,128},{3,129},{4,256},{5,257},{6,384},{7,385},{8,8},... | collective-permute-start | bytes 294920 | tf_op jit(solution)/shard_map/ppermute | solution.py:213
  6.1 7.0 %collective-permute-done.9 = bf16[64,768]{1,0:T(8,128)(2,1)S(1)} collective-permute-done((bf16[64,768]{1,0:T(8,128)(2,1)}, bf16[64,768]{1,0:T(8,128)(2,1)S(1)}, u32[]{:S(2)}, u32[]{:S(2)}) %collective-permute-start.9) | collective-permute-done | bytes 98336 | tf_op jit(solution)/shard_map/ppermute | solution.py:213
  13.1 32.6 %all-gather.3 = bf16[512,768]{1,0:T(8,128)(2,1)S(1)} all-gather(bf16[64,768]{1,0:T(8,128)(2,1)S(1)} %collective-permute-done.9), channel_id=5, replica_groups={{0,16,32,48,64,80,96,112},{8,24,40,56,72,88,104,120},{128,144,160,176,1..., dimensions={0}, use_global_device_ids=true | all-gather | bytes 884736 | tf_op jit(solution)/shard_map/all_gather | solution.py:197
  45.7 2.0 %collective-permute-start.10 = (bf16[512,768]{1,0:T(8,128)(2,1)S(1)}, bf16[512,768]{1,0:T(8,128)(2,1)S(1)}, u32[]{:S(2)}, u32[]{:S(2)}) collective-permute-start(bf16[512,768]{1,0:T(8,128)(2,1)S(1)} %all-gather.3), channel_id=1, source_target_pairs={{0,8},{8,0},{16,24},{24,16},{32,40},{40,32},{48,56},{56,48},{64,72... | collective-permute-start | bytes 2359304 | tf_op jit(solution)/shard_map/ppermute | solution.py:215
  47.7 0.1 constant_dynamic-update-slice_fusion.1
  47.8 2.2 %collective-permute-done.10 = bf16[512,768]{1,0:T(8,128)(2,1)S(1)} collective-permute-done((bf16[512,768]{1,0:T(8,128)(2,1)S(1)}, bf16[512,768]{1,0:T(8,128)(2,1)S(1)}, u32[]{:S(2)}, u32[]{:S(2)}) %collective-permute-start.10) | collective-permute-done | bytes 786464 | tf_op jit(solution)/shard_map/ppermute | solution.py:215
  50.0 0.1 constant_dynamic-update-slice_fusion.refs_0_
  50.0 1.9 %collective-permute-start.11 = (bf16[1024,768]{1,0:T(8,128)(2,1)S(1)}, bf16[1024,768]{1,0:T(8,128)(2,1)S(1)}, u32[]{:S(2)}, u32[]{:S(2)}) collective-permute-start(bf16[1024,768]{1,0:T(8,128)(2,1)S(1)} %constant_dynamic-update-slice_fusion.refs_0_), channel_id=1, source_target_pairs={{0,128},{8,392},{16,144},{24,408},{32,160},{40,424},{48,176},{56,4... | collective-permute-start | bytes 4718600 | tf_op jit(solution)/shard_map/ppermute | solution.py:216
  52.0 0.7 fusion.5
  52.7 3.0 %collective-permute-start.1 = (bf16[2,256,128]{2,1,0:T(8,128)(2,1)}, bf16[2,256,128]{2,1,0:T(8,128)(2,1)S(1)}, u32[]{:S(2)}, u32[]{:S(2)}) collective-permute-start(bf16[2,256,128]{2,1,0:T(8,128)(2,1)} %get-tuple-element.18.own), channel_id=1, source_target_pairs={{0,16},{8,24},{16,32},{24,40},{32,48},{40,56},{48,64},{56,72},{64,... | collective-permute-start | bytes 393224 | tf_op jit(solution)/shard_map/ppermute | solution.py:208
  55.7 7.4 %collective-permute-done.1.o1 = bf16[2,256,128]{2,1,0:T(8,128)(2,1)S(1)} collective-permute-done((bf16[2,256,128]{2,1,0:T(8,128)(2,1)}, bf16[2,256,128]{2,1,0:T(8,128)(2,1)S(1)}, u32[]{:S(2)}, u32[]{:S(2)}) %collective-permute-start.1) | collective-permute-done | bytes 131104 | tf_op jit(solution)/shard_map/ppermute | solution.py:208
  63.1 0.7 pad_maximum_fusion.1
  63.8 1.9 %collective-permute-start.2 = (bf16[2,2,256,128]{3,2,1,0:T(8,128)(2,1)}, bf16[2,2,256,128]{3,2,1,0:T(8,128)(2,1)S(1)}, u32[]{:S(2)}, u32[]{:S(2)}) collective-permute-start(bf16[2,2,256,128]{3,2,1,0:T(8,128)(2,1)} %pad_maximum_fusion.1), channel_id=1, source_target_pairs={{0,32},{8,40},{16,48},{24,56},{32,64},{40,72},{48,80},{56,88},{64,... | collective-permute-start | bytes 786440 | tf_op jit(solution)/shard_map/ppermute | solution.py:210
  65.7 1.9 %collective-permute-start = (bf16[2,256,128]{2,1,0:T(8,128)(2,1)}, bf16[2,256,128]{2,1,0:T(8,128)(2,1)}, u32[]{:S(2)}, u32[]{:S(2)}) collective-permute-start(bf16[2,256,128]{2,1,0:T(8,128)(2,1)} %get-tuple-element.18.own), channel_id=1, source_target_pairs={{0,8},{16,24},{32,40},{48,56},{64,72},{80,88},{96,104},{112,120},{... | collective-permute-start | bytes 393224 | tf_op jit(solution)/shard_map/ppermute | solution.py:209
  67.7 0.1 stack.45.me
  67.8 15.1 %collective-permute-done.2.o23 = bf16[2,2,256,128]{3,2,1,0:T(8,128)(2,1)S(1)} collective-permute-done((bf16[2,2,256,128]{3,2,1,0:T(8,128)(2,1)}, bf16[2,2,256,128]{3,2,1,0:T(8,128)(2,1)S(1)}, u32[]{:S(2)}, u32[]{:S(2)}) %collective-permute-start.2) | collective-permute-done | bytes 262176 | tf_op jit(solution)/shard_map/ppermute | solution.py:210
  82.9 0.0 copy-start.3
  82.9 0.0 copy-start.4
  83.0 0.0 copy-start.5
  83.0 0.0 copy-start.6
  83.0 2.5 %all-gather = bf16[6,2,256,128]{3,2,1,0:T(8,128)(2,1)S(1)} all-gather(bf16[3,2,256,128]{3,2,1,0:T(8,128)(2,1)S(1)} %pad_maximum_fusion), channel_id=2, replica_groups={{0,8},{16,24},{32,40},{48,56},{64,72},{80,88},{96,104},{112,120},{128,1..., dimensions={0}, use_global_device_ids=true | all-gather | bytes 1179648 | tf_op jit(solution)/shard_map/all_gather | solution.py:197
  85.5 0.0 collective-permute-done.11.refs_1_
  85.5 0.1 slice.36
  85.5 4.0 %collective-permute-start.13 = (bf16[512,768]{1,0:T(8,128)(2,1)S(1)}, bf16[512,768]{1,0:T(8,128)(2,1)}, u32[]{:S(2)}, u32[]{:S(2)}) collective-permute-start(bf16[512,768]{1,0:T(8,128)(2,1)S(1)} %slice.36), channel_id=1, source_target_pairs={{0,128},{8,392},{16,144},{24,408},{32,160},{40,424},{48,176},{56,4... | collective-permute-start | bytes 2359304 | tf_op jit(solution)/shard_map/ppermute | solution.py:217
  89.6 1.9 %collective-permute-start.12 = (bf16[1024,768]{1,0:T(8,128)(2,1)S(1)}, bf16[1024,768]{1,0:T(8,128)(2,1)}, u32[]{:S(2)}, u32[]{:S(2)}) collective-permute-start(bf16[1024,768]{1,0:T(8,128)(2,1)S(1)} %collective-permute-done.11.refs_1_), channel_id=1, source_target_pairs={{0,8},{8,0},{16,24},{24,16},{32,40},{40,32},{48,56},{56,48},{64,72... | collective-permute-start | bytes 4718600 | tf_op jit(solution)/shard_map/ppermute | solution.py:218
  91.5 0.0 collective-permute-done.last
  91.6 8.9 %shard_map.73 = (bf16[256,512]{1,0:T(8,128)(2,1)S(1)}, f32[4,2,256,128]{3,2,1,0:T(8,128)S(1)}, bf16[2,256,128]{2,1,0:T(8,128)(2,1)}, bf16[3,2,256,128]{3,2,1,0:T(8,128)(2,1)S(1)}) custom-call(s32[6]{0:T(128)S(1)} %stack.45.me, s32[64]{0:T(128)S(1)} %copy-done.6, bf16[256,512]{1,0:T(8,128)(2,1)S(1)} %copy-done.3, bf16[256,512]{1,0:T(8,128)(2,1)S(1)} %copy-done.4, ...), custom_call_target="tpu_custom_call" | custom-call | flops 2700000000 | bytes 5000000 | tf_op jit(solution)/shard_map/pallas_call | solution.py:181
  100.5 2.5 %all-gather.1 = bf16[6,2,256,128]{3,2,1,0:T(8,128)(2,1)S(1)} all-gather(bf16[3,2,256,128]{3,2,1,0:T(8,128)(2,1)S(1)} %get-tuple-element.12), channel_id=3, replica_groups={{0,8},{16,24},{32,40},{48,56},{64,72},{80,88},{96,104},{112,120},{128,1..., dimensions={0}, use_global_device_ids=true | all-gather | bytes 1179648 | tf_op jit(solution)/shard_map/all_gather | solution.py:197
  103.0 0.1 fusion.1
  103.1 1.9 %collective-permute-start.3 = (bf16[2,2,256,128]{3,2,1,0:T(8,128)(2,1)S(1)}, bf16[2,2,256,128]{3,2,1,0:T(8,128)(2,1)S(1)}, u32[]{:S(2)}, u32[]{:S(2)}) collective-permute-start(bf16[2,2,256,128]{3,2,1,0:T(8,128)(2,1)S(1)} %fusion.1), channel_id=1, source_target_pairs={{0,480},{8,488},{16,496},{24,504},{32,0},{40,8},{48,16},{56,24},{6... | collective-permute-start | bytes 786440 | tf_op jit(solution)/shard_map/ppermute | solution.py:236
  105.0 2.9 %collective-permute-start.5 = (bf16[2,256,128]{2,1,0:T(8,128)(2,1)}, bf16[2,256,128]{2,1,0:T(8,128)(2,1)S(1)}, u32[]{:S(2)}, u32[]{:S(2)}) collective-permute-start(bf16[2,256,128]{2,1,0:T(8,128)(2,1)} %get-tuple-element.13), channel_id=1, source_target_pairs={{8,0},{24,16},{40,32},{56,48},{72,64},{88,80},{104,96},{120,112},{... | collective-permute-start | bytes 393224 | tf_op jit(solution)/shard_map/ppermute | solution.py:237
  107.9 0.0 collective-permute-done.13.refs_3_
  107.9 1.9 %collective-permute-start.14 = (bf16[512,768]{1,0:T(8,128)(2,1)}, bf16[512,768]{1,0:T(8,128)(2,1)}, u32[]{:S(2)}, u32[]{:S(2)}) collective-permute-start(bf16[512,768]{1,0:T(8,128)(2,1)} %collective-permute-done.13.refs_3_), channel_id=1, source_target_pairs={{0,8},{8,0},{16,24},{24,16},{32,40},{40,32},{48,56},{56,48},{64,72... | collective-permute-start | bytes 2359304 | tf_op jit(solution)/shard_map/ppermute | solution.py:218
  109.9 8.9 %collective-permute-done.3 = bf16[2,2,256,128]{3,2,1,0:T(8,128)(2,1)S(1)} collective-permute-done((bf16[2,2,256,128]{3,2,1,0:T(8,128)(2,1)S(1)}, bf16[2,2,256,128]{3,2,1,0:T(8,128)(2,1)S(1)}, u32[]{:S(2)}, u32[]{:S(2)}) %collective-permute-start.3) | collective-permute-done | bytes 262176 | tf_op jit(solution)/shard_map/ppermute | solution.py:236
  118.8 0.8 fusion.2
  119.5 1.9 %collective-permute-start.4 = (bf16[2,256,128]{2,1,0:T(8,128)(2,1)}, bf16[2,256,128]{2,1,0:T(8,128)(2,1)}, u32[]{:S(2)}, u32[]{:S(2)}) collective-permute-start(bf16[2,256,128]{2,1,0:T(8,128)(2,1)} %fusion.2), channel_id=1, source_target_pairs={{0,496},{8,504},{16,0},{24,8},{32,16},{40,24},{48,32},{56,40},{64,... | collective-permute-start | bytes 393224 | tf_op jit(solution)/shard_map/ppermute | solution.py:239
  121.5 7.3 %collective-permute-start.8 = (bf16[256,512]{1,0:T(8,128)(2,1)}, bf16[256,512]{1,0:T(8,128)(2,1)S(1)}, u32[]{:S(2)}, u32[]{:S(2)}) collective-permute-start(bf16[256,512]{1,0:T(8,128)(2,1)} %copy-done.1), channel_id=1, source_target_pairs={{0,2},{1,3},{2,4},{3,5},{4,6},{5,7},{6,0},{7,1},{8,10},{9,11},{10,... | collective-permute-start | bytes 786440 | tf_op jit(solution)/shard_map/ppermute | solution.py:244
  128.8 0.0 collective-permute-done.5
  128.8 4.7 %collective-permute-start.7 = (bf16[256,512]{1,0:T(8,128)(2,1)}, bf16[256,512]{1,0:T(8,128)(2,1)S(1)}, u32[]{:S(2)}, u32[]{:S(2)}) collective-permute-start(bf16[256,512]{1,0:T(8,128)(2,1)} %copy-done.1), channel_id=1, source_target_pairs={{0,4},{1,5},{2,6},{3,7},{4,0},{5,1},{6,2},{7,3},{8,12},{9,13},{10,... | collective-permute-start | bytes 786440 | tf_op jit(solution)/shard_map/ppermute | solution.py:244
  133.5 0.0 collective-permute-done.4
  133.5 3.1 %collective-permute-start.6 = (bf16[256,512]{1,0:T(8,128)(2,1)}, bf16[256,512]{1,0:T(8,128)(2,1)S(1)}, u32[]{:S(2)}, u32[]{:S(2)}) collective-permute-start(bf16[256,512]{1,0:T(8,128)(2,1)} %copy-done.1), channel_id=1, source_target_pairs={{0,6},{1,7},{2,0},{3,1},{4,2},{5,3},{6,4},{7,5},{8,14},{9,15},{10,... | collective-permute-start | bytes 786440 | tf_op jit(solution)/shard_map/ppermute | solution.py:244
  136.7 1.2 fusion.4
  137.9 35.8 %all-gather.2 = bf16[8,256,128]{2,1,0:T(8,128)(2,1)S(1)} all-gather(bf16[2,256,128]{2,1,0:T(8,128)(2,1)S(1)} %fusion.4), channel_id=4, replica_groups={{0,2,4,6},{1,3,5,7},{8,10,12,14},{9,11,13,15},{16,18,20,22},{17,19,21,2..., dimensions={0}, use_global_device_ids=true | all-gather | bytes 655360 | tf_op jit(solution)/shard_map/all_gather | solution.py:197
  173.7 0.0 collective-permute-done.12.refs_2_
  173.7 3.1 %shard_map.74.acc_in = f32[2,256,512]{2,1,0:T(8,128)S(1)} custom-call(s32[6]{0:T(128)S(1)} %stack.45.me, bf16[256,512]{1,0:T(8,128)(2,1)S(1)} %copy-done.2, bf16[256,512]{1,0:T(8,128)(2,1)S(1)} %collective-permute-done.6.d1, bf16[256,512]{1,0:T(8,128)(2,1)S(1)} %collective-permute-done.7.d2, bf16[256,512]{1,0:T(8,128)(2,1)S(1)} %collective-permute-done.8.d3, ...), custom_call_target="tpu_custom_call" | custom-call | flops 1073741824 | bytes 6000000 | tf_op jit(solution)/shard_map/pallas_call | solution.py:181
  176.9 3.0 %shard_map.75 = (bf16[256,512]{1,0:T(8,128)(2,1)S(1)}, f32[256,512]{1,0:T(8,128)S(1)}) custom-call(s32[6]{0:T(128)S(1)} %stack.45.me, bf16[4,2,256,128]{3,2,1,0:T(8,128)(2,1)S(1)} %bitcast.42, f32[2,256,512]{2,1,0:T(8,128)S(1)} %shard_map.74.acc_in, bf16[1024,768]{1,0:T(8,128)(2,1)S(1)} %constant_dynamic-update-slice_fusion.refs_0_, ...), custom_call_target="tpu_custom_call" | custom-call | flops 536870912 | bytes 4000000 | tf_op jit(solution)/shard_map/pallas_call | solution.py:181
  179.9 7.4 %all-gather.4 = bf16[512,512]{1,0:T(8,128)(2,1)S(1)} all-gather(bf16[256,512]{1,0:T(8,128)(2,1)S(1)} %get-tuple-element.16), channel_id=6, replica_groups={{0,1},{2,3},{4,5},{6,7},{8,9},{10,11},{12,13},{14,15},{16,17},{18,19},{..., dimensions={0}, use_global_device_ids=true | all-gather | bytes 786432 | tf_op jit(solution)/shard_map/all_gather | solution.py:197
  187.3 0.8 fusion
  (23 shorter events, 0.1 us)
Async XLA Ops:
  0.0 13.1 %collective-permute-start.9 = (bf16[64,768]{1,0:T(8,128)(2,1)}, bf16[64,768]{1,0:T(8,128)(2,1)S(1)}, u32[]{:S(2)}, u32[]{:S(2)}) collective-permute-start(bf16[64,768]{1,0:T(8,128)(2,1)} %bitcast.51), channel_id=1, source_target_pairs={{0,0},{1,1},{2,128},{3,129},{4,256},{5,257},{6,384},{7,385},{8,8},... | collective-permute-start | bytes 294920 | tf_op jit(solution)/shard_map/ppermute | solution.py:213
  45.7 6.3 %copy-start.9 = (bf16[256,128]{1,0:T(8,128)(2,1)S(1)}, bf16[256,128]{1,0:T(8,128)(2,1)}, u32[]{:S(2)}) copy-start(bf16[256,128]{1,0:T(8,128)(2,1)} %param.9) | copy-start | bytes 196612
  45.7 6.3 %copy-start.10 = (bf16[256,128]{1,0:T(8,128)(2,1)S(1)}, bf16[256,128]{1,0:T(8,128)(2,1)}, u32[]{:S(2)}) copy-start(bf16[256,128]{1,0:T(8,128)(2,1)} %param.8) | copy-start | bytes 196612
  45.7 4.3 %collective-permute-start.10 = (bf16[512,768]{1,0:T(8,128)(2,1)S(1)}, bf16[512,768]{1,0:T(8,128)(2,1)S(1)}, u32[]{:S(2)}, u32[]{:S(2)}) collective-permute-start(bf16[512,768]{1,0:T(8,128)(2,1)S(1)} %all-gather.3), channel_id=1, source_target_pairs={{0,8},{8,0},{16,24},{24,16},{32,40},{40,32},{48,56},{56,48},{64,72... | collective-permute-start | bytes 2359304 | tf_op jit(solution)/shard_map/ppermute | solution.py:215
  50.0 35.4 %collective-permute-start.11 = (bf16[1024,768]{1,0:T(8,128)(2,1)S(1)}, bf16[1024,768]{1,0:T(8,128)(2,1)S(1)}, u32[]{:S(2)}, u32[]{:S(2)}) collective-permute-start(bf16[1024,768]{1,0:T(8,128)(2,1)S(1)} %constant_dynamic-update-slice_fusion.refs_0_), channel_id=1, source_target_pairs={{0,128},{8,392},{16,144},{24,408},{32,160},{40,424},{48,176},{56,4... | collective-permute-start | bytes 4718600 | tf_op jit(solution)/shard_map/ppermute | solution.py:216
  52.7 10.4 %collective-permute-start.1 = (bf16[2,256,128]{2,1,0:T(8,128)(2,1)}, bf16[2,256,128]{2,1,0:T(8,128)(2,1)S(1)}, u32[]{:S(2)}, u32[]{:S(2)}) collective-permute-start(bf16[2,256,128]{2,1,0:T(8,128)(2,1)} %get-tuple-element.18.own), channel_id=1, source_target_pairs={{0,16},{8,24},{16,32},{24,40},{32,48},{40,56},{48,64},{56,72},{64,... | collective-permute-start | bytes 393224 | tf_op jit(solution)/shard_map/ppermute | solution.py:208
  63.8 19.1 %collective-permute-start.2 = (bf16[2,2,256,128]{3,2,1,0:T(8,128)(2,1)}, bf16[2,2,256,128]{3,2,1,0:T(8,128)(2,1)S(1)}, u32[]{:S(2)}, u32[]{:S(2)}) collective-permute-start(bf16[2,2,256,128]{3,2,1,0:T(8,128)(2,1)} %pad_maximum_fusion.1), channel_id=1, source_target_pairs={{0,32},{8,40},{16,48},{24,56},{32,64},{40,72},{48,80},{56,88},{64,... | collective-permute-start | bytes 786440 | tf_op jit(solution)/shard_map/ppermute | solution.py:210
  65.7 25.8 %collective-permute-start = (bf16[2,256,128]{2,1,0:T(8,128)(2,1)}, bf16[2,256,128]{2,1,0:T(8,128)(2,1)}, u32[]{:S(2)}, u32[]{:S(2)}) collective-permute-start(bf16[2,256,128]{2,1,0:T(8,128)(2,1)} %get-tuple-element.18.own), channel_id=1, source_target_pairs={{0,8},{16,24},{32,40},{48,56},{64,72},{80,88},{96,104},{112,120},{... | collective-permute-start | bytes 393224 | tf_op jit(solution)/shard_map/ppermute | solution.py:209
  82.9 8.6 %copy-start.3 = (bf16[256,512]{1,0:T(8,128)(2,1)S(1)}, bf16[256,512]{1,0:T(8,128)(2,1)}, u32[]{:S(2)}) copy-start(bf16[256,512]{1,0:T(8,128)(2,1)} %q_ref.1) | copy-start | bytes 786436
  82.9 8.6 %copy-start.4 = (bf16[256,512]{1,0:T(8,128)(2,1)S(1)}, bf16[256,512]{1,0:T(8,128)(2,1)}, u32[]{:S(2)}) copy-start(bf16[256,512]{1,0:T(8,128)(2,1)} %do_ref.1) | copy-start | bytes 786436
  83.0 8.6 %copy-start.5 = (bf16[256,512]{1,0:T(8,128)(2,1)S(1)}, bf16[256,512]{1,0:T(8,128)(2,1)}, u32[]{:S(2)}) copy-start(bf16[256,512]{1,0:T(8,128)(2,1)} %out_ref.1) | copy-start | bytes 786436
  83.0 8.6 %copy-start.6 = (s32[64]{0:T(128)S(1)}, s32[64]{0:T(128)}, u32[]{:S(2)}) copy-start(s32[64]{0:T(128)} %lengths.1) | copy-start | bytes 772
  85.5 22.4 %collective-permute-start.13 = (bf16[512,768]{1,0:T(8,128)(2,1)S(1)}, bf16[512,768]{1,0:T(8,128)(2,1)}, u32[]{:S(2)}, u32[]{:S(2)}) collective-permute-start(bf16[512,768]{1,0:T(8,128)(2,1)S(1)} %slice.36), channel_id=1, source_target_pairs={{0,128},{8,392},{16,144},{24,408},{32,160},{40,424},{48,176},{56,4... | collective-permute-start | bytes 2359304 | tf_op jit(solution)/shard_map/ppermute | solution.py:217
  89.6 84.1 %collective-permute-start.12 = (bf16[1024,768]{1,0:T(8,128)(2,1)S(1)}, bf16[1024,768]{1,0:T(8,128)(2,1)}, u32[]{:S(2)}, u32[]{:S(2)}) collective-permute-start(bf16[1024,768]{1,0:T(8,128)(2,1)S(1)} %collective-permute-done.11.refs_1_), channel_id=1, source_target_pairs={{0,8},{8,0},{16,24},{24,16},{32,40},{40,32},{48,56},{56,48},{64,72... | collective-permute-start | bytes 4718600 | tf_op jit(solution)/shard_map/ppermute | solution.py:218
  100.5 18.2 %copy-start = (f32[4,2,256,128]{3,2,1,0:T(8,128)}, f32[4,2,256,128]{3,2,1,0:T(8,128)S(1)}, u32[]{:S(2)}) copy-start(f32[4,2,256,128]{3,2,1,0:T(8,128)S(1)} %get-tuple-element.11) | copy-start | bytes 3145732
  100.5 19.0 %copy-start.1 = (bf16[256,512]{1,0:T(8,128)(2,1)}, bf16[256,512]{1,0:T(8,128)(2,1)S(1)}, u32[]{:S(2)}) copy-start(bf16[256,512]{1,0:T(8,128)(2,1)S(1)} %get-tuple-element.14.d0) | copy-start | bytes 786436
  103.1 15.6 %collective-permute-start.3 = (bf16[2,2,256,128]{3,2,1,0:T(8,128)(2,1)S(1)}, bf16[2,2,256,128]{3,2,1,0:T(8,128)(2,1)S(1)}, u32[]{:S(2)}, u32[]{:S(2)}) collective-permute-start(bf16[2,2,256,128]{3,2,1,0:T(8,128)(2,1)S(1)} %fusion.1), channel_id=1, source_target_pairs={{0,480},{8,488},{16,496},{24,504},{32,0},{40,8},{48,16},{56,24},{6... | collective-permute-start | bytes 786440 | tf_op jit(solution)/shard_map/ppermute | solution.py:236
  105.0 23.7 %collective-permute-start.5 = (bf16[2,256,128]{2,1,0:T(8,128)(2,1)}, bf16[2,256,128]{2,1,0:T(8,128)(2,1)S(1)}, u32[]{:S(2)}, u32[]{:S(2)}) collective-permute-start(bf16[2,256,128]{2,1,0:T(8,128)(2,1)} %get-tuple-element.13), channel_id=1, source_target_pairs={{8,0},{24,16},{40,32},{56,48},{72,64},{88,80},{104,96},{120,112},{... | collective-permute-start | bytes 393224 | tf_op jit(solution)/shard_map/ppermute | solution.py:237
  107.9 65.7 %collective-permute-start.14 = (bf16[512,768]{1,0:T(8,128)(2,1)}, bf16[512,768]{1,0:T(8,128)(2,1)}, u32[]{:S(2)}, u32[]{:S(2)}) collective-permute-start(bf16[512,768]{1,0:T(8,128)(2,1)} %collective-permute-done.13.refs_3_), channel_id=1, source_target_pairs={{0,8},{8,0},{16,24},{24,16},{32,40},{40,32},{48,56},{56,48},{64,72... | collective-permute-start | bytes 2359304 | tf_op jit(solution)/shard_map/ppermute | solution.py:218
  118.8 0.8 copy-start.7
  119.5 14.0 %collective-permute-start.4 = (bf16[2,256,128]{2,1,0:T(8,128)(2,1)}, bf16[2,256,128]{2,1,0:T(8,128)(2,1)}, u32[]{:S(2)}, u32[]{:S(2)}) collective-permute-start(bf16[2,256,128]{2,1,0:T(8,128)(2,1)} %fusion.2), channel_id=1, source_target_pairs={{0,496},{8,504},{16,0},{24,8},{32,16},{40,24},{48,32},{56,40},{64,... | collective-permute-start | bytes 393224 | tf_op jit(solution)/shard_map/ppermute | solution.py:239
  121.5 52.2 %copy-start.2 = (bf16[256,512]{1,0:T(8,128)(2,1)S(1)}, bf16[256,512]{1,0:T(8,128)(2,1)}, u32[]{:S(2)}) copy-start(bf16[256,512]{1,0:T(8,128)(2,1)} %copy-done.1) | copy-start | bytes 786436
  121.5 52.2 %collective-permute-start.8 = (bf16[256,512]{1,0:T(8,128)(2,1)}, bf16[256,512]{1,0:T(8,128)(2,1)S(1)}, u32[]{:S(2)}, u32[]{:S(2)}) collective-permute-start(bf16[256,512]{1,0:T(8,128)(2,1)} %copy-done.1), channel_id=1, source_target_pairs={{0,2},{1,3},{2,4},{3,5},{4,6},{5,7},{6,0},{7,1},{8,10},{9,11},{10,... | collective-permute-start | bytes 786440 | tf_op jit(solution)/shard_map/ppermute | solution.py:244
  128.8 4.7 %copy-start.8 = (bf16[2,256,128]{2,1,0:T(8,128)(2,1)}, bf16[2,256,128]{2,1,0:T(8,128)(2,1)S(1)}, u32[]{:S(2)}) copy-start(bf16[2,256,128]{2,1,0:T(8,128)(2,1)S(1)} %collective-permute-done.5) | copy-start | bytes 393220
  128.8 44.9 %collective-permute-start.7 = (bf16[256,512]{1,0:T(8,128)(2,1)}, bf16[256,512]{1,0:T(8,128)(2,1)S(1)}, u32[]{:S(2)}, u32[]{:S(2)}) collective-permute-start(bf16[256,512]{1,0:T(8,128)(2,1)} %copy-done.1), channel_id=1, source_target_pairs={{0,4},{1,5},{2,6},{3,7},{4,0},{5,1},{6,2},{7,3},{8,12},{9,13},{10,... | collective-permute-start | bytes 786440 | tf_op jit(solution)/shard_map/ppermute | solution.py:244
  133.5 40.2 %collective-permute-start.6 = (bf16[256,512]{1,0:T(8,128)(2,1)}, bf16[256,512]{1,0:T(8,128)(2,1)S(1)}, u32[]{:S(2)}, u32[]{:S(2)}) collective-permute-start(bf16[256,512]{1,0:T(8,128)(2,1)} %copy-done.1), channel_id=1, source_target_pairs={{0,6},{1,7},{2,0},{3,1},{4,2},{5,3},{6,4},{7,5},{8,14},{9,15},{10,... | collective-permute-start | bytes 786440 | tf_op jit(solution)/shard_map/ppermute | solution.py:244
where the time goes:
time: 189 us; the launch traced here: 188 us
  blocking collectives  80.9 us (43%)
  starting transfers between devices  46.6 us (25%)
  waiting for transfers between devices  40.5 us (21%)
  Pallas kernels  15.1 us (8%)
  other arithmetic  4.24 us (2%)
    all_gather x5, blocking collectives, gather(): return lax.all_gather(array, axis, axis=0, axis_index_groups=groups)  80.9 us
    ppermute x3, starting transfers between devices, step(): lax.ppermute(dq, 'head', head_shift(-2 * r))  15.1 us
    pallas_call x3, Pallas kernels, call(): pl.pallas_call(kernel, out_shape=outs, in_specs=[smem] * n_scalar + [vmem...  15.1 us
    ppermute x1, waiting for transfers between devices, step(): o23 = lax.ppermute(jnp.stack([own, o1]), 'ctx', chip_shift(2))  15.1 us
    ppermute x1, waiting for transfers between devices, step(): far_back = lax.ppermute(far, 'ctx', chip_shift(-2))  8.89 us
    ppermute x1, waiting for transfers between devices, step(): o1 = lax.ppermute(own, 'ctx', chip_shift(1))  7.38 us
    ppermute x1, waiting for transfers between devices, step(): lax.ppermute(proj_weight.reshape(64, 768), ('ctx', 'head'), WEIGHT_TRANSP...  6.98 us
    ppermute x1, starting transfers between devices, step(): lax.ppermute(proj_weight.reshape(64, 768), ('ctx', 'head'), WEIGHT_TRANSP...  6.06 us
  transfers between devices with their start and end apart: 15, of which 5 were waited for; matrix products, arithmetic and copies ran while one was open for 2% of the time, Pallas kernels for 5%

commit v1 on v0

--- a/solution.py
+++ b/solution.py
@@ -14,6 +14,7 @@
 NCHIP = NX * NZ
 NHEAD = 8
 SLOTS = 8
+Z_ORDER = (0, 2, 4, 6, 7, 1, 3, 5)
 DOCS = 64
 LOG2E = 1.4426950408889634
 SCALE = HD ** (-0.5)
@@ -29,7 +30,13 @@
     return [(2 * q + c, 2 * ((q + by) % NCHIP) + c) for q in range(NCHIP) for c in range(2)]
 
 
-Z_RINGS = [[ctx_of(x, z, c) for z in range(NZ)] for x in range(NX) for c in range(2)]
+def z_shift(by):
+    return [
+        (ctx_of(x, z, c), ctx_of(x, z + by, c))
+        for x in range(NX) for z in range(NZ) for c in range(2)
+    ]
+
+
 X_SPLIT = [
     (ctx_of(x, z, c), ctx_of(x + 1 - 2 * c, z, c))
     for x in range(NX) for z in range(NZ) for c in range(2)
@@ -53,7 +60,6 @@
     return [(j, (j + by) % NHEAD) for j in range(NHEAD)]
 
 
-SAME_PARITY = [[b + 2 * a for a in range(4)] for b in range(2)]
 HEAD_PAIRS = [[2 * k, 2 * k + 1] for k in range(4)]
 
 NT = (((1,), (1,)), ((), ()))
@@ -134,36 +140,27 @@
         dq_ref[:, h * HD:(h + 1) * HD] = dq[h].astype(BF16)
 
 
-def project(me, heads, blocks, cols, acc_ref):
-    x, core = me[1], me[3]
+FIRST, SECOND = slice(0, 512), slice(512, 1024)
+
+
+def proj_kernel(
+    me, d0, d1, d2, d3, k0, k1, k2, k3, own, near, other, last,
+    send_ref, keep_ref, heads, acc_ref, full,
+):
+    x, core, k, b = me[1], me[3], me[4], me[5]
+    for r, (d, kv) in enumerate(((d0, k0), (d1, k1), (d2, k2), (d3, k3))):
+        a = (k + r) % NX
+        heads[a, :, :512] = d[...]
+        heads[a, :, 512:640] = kv[0]
+        heads[a, :, 640:] = kv[1]
     up = 1 - 2 * core
-    own, near, other, half, rest = blocks
-    first, second = slice(0, 512), slice(512, 1024)
     here, behind, ahead = heads[x], heads[(x - up + NX) % NX], heads[(x + up + NX) % NX]
     far = heads[(x + 2) % NX]
-    for side, rows, swapped, last in ((0, first, second, half), (1, second, first, rest)):
+    for side, rows, swapped in ((0, FIRST, SECOND), (1, SECOND, FIRST)):
         acc_ref[side] = (
-            acc_ref[side] + dot(here, own[rows, cols], NT) + dot(behind, near[rows, cols], NT)
-            + dot(ahead, other[swapped, cols], NT) + dot(far, last[:, cols], NT)
+            dot(here, own[rows, :], NT) + dot(behind, near[rows, :], NT)
+            + dot(ahead, other[swapped, :], NT) + dot(far, last[rows, :], NT)
         )
-
-
-def proj_q_kernel(me, d0, d1, d2, d3, *refs):
-    blocks, (acc_ref, heads) = refs[:5], refs[5:]
-    for r, d in enumerate((d0, d1, d2, d3)):
-        heads[(me[4] + r) % NX] = d[...]
-    acc_ref[...] = jnp.zeros_like(acc_ref)
-    project(me, heads, blocks, slice(0, 512), acc_ref)
-
-
-def proj_kv_kernel(me, kv_ref, acc_in, *refs):
-    blocks, (send_ref, keep_ref, heads, acc_ref, full) = refs[:5], refs[5:]
-    core, b = me[3], me[5]
-    for a in range(NX):
-        heads[a, :, :HD] = kv_ref[a, 0]
-        heads[a, :, HD:] = kv_ref[a, 1]
-    acc_ref[...] = acc_in[...]
-    project(me, heads, blocks, slice(512, 768), acc_ref)
     left = lax.broadcasted_iota(jnp.int32, (TILE, 128), 1) < 64
     for n in range(4):
         lanes = slice(128 * n, 128 * n + 128)
@@ -175,7 +172,7 @@
     keep_ref[...] = full[b]
 
 
-def call(kernel, n_scalar, args, outs, scratch=(), flops=0, nbytes=0, mib=8):
+def call(kernel, n_scalar, args, outs, scratch=(), flops=0, nbytes=0, mib=6):
     vmem = pl.BlockSpec(memory_space=pltpu.VMEM)
     smem = pl.BlockSpec(memory_space=pltpu.SMEM)
     return pl.pallas_call(
@@ -197,6 +194,14 @@
     return lax.all_gather(array, axis, axis=0, axis_index_groups=groups)
 
 
+def in_order(w, z):
+    out = w
+    for slot, dz in enumerate(Z_ORDER):
+        piece = w[64 * slot:64 * slot + 64]
+        out = lax.dynamic_update_slice_in_dim(out, piece, (z + dz) % NZ * 64, 0)
+    return out
+
+
 def step(queries, keys, values, out_grad, attn_out, lengths, proj_weight):
     i = lax.axis_index("ctx")
     j = lax.axis_index("head")
@@ -211,11 +216,13 @@
     both = gather(jnp.concatenate([o1[None], o23]), "ctx", CORES)
 
     w = lax.ppermute(proj_weight.reshape(64, 768), ("ctx", "head"), WEIGHT_TRANSPOSE)
-    w = gather(w, "ctx", Z_RINGS).reshape(512, 768)
+    for by in (-2, -4, 1):
+        w = jnp.concatenate([w, lax.ppermute(w, "ctx", z_shift(by))])
+    w = in_order(w, chip % NZ)
     w = jnp.concatenate([w, lax.ppermute(w, "ctx", CORE_SWAP)])
     w1 = lax.ppermute(w, "ctx", X_SPLIT)
-    w2 = lax.ppermute(w1[:512], "ctx", X_SPLIT)
-    weights = [w, w1, lax.ppermute(w1, "ctx", CORE_SWAP), w2, lax.ppermute(w2, "ctx", CORE_SWAP)]
+    w2 = lax.ppermute(w1, "ctx", X_SPLIT)
+    weights = [w, w1, lax.ppermute(w1, "ctx", CORE_SWAP), w2]
 
     dq, g_own, g_last, g_x = call(
         attention_kernel, 2,
@@ -227,7 +234,7 @@
             sds((3, 2, TILE, HD), BF16),
         ),
         scratch=[pltpu.VMEM((SLOTS * TILE, GROUP * TILE), F32)],
-        flops=2_700_000_000, nbytes=5_000_000, mib=18,
+        flops=2_700_000_000, nbytes=5_000_000, mib=10,
     )
 
     swapped = gather(g_x, "ctx", CORES)
@@ -242,17 +249,15 @@
     ).astype(BF16)
 
     dqs = [dq] + [lax.ppermute(dq, "head", head_shift(-2 * r)) for r in (1, 2, 3)]
-    acc = call(
-        proj_q_kernel, 1, [me] + dqs + weights, sds((2, TILE, 512), F32),
-        scratch=[pltpu.VMEM((NX, TILE, 512), BF16)],
-        flops=1_073_741_824, nbytes=6_000_000,
-    )
-    kvs = gather(kv, "head", SAME_PARITY)
+    kvs = [kv] + [lax.ppermute(kv, "head", head_shift(-2 * r)) for r in (1, 2, 3)]
     send, keep = call(
-        proj_kv_kernel, 1, [me, kvs, acc] + weights,
+        proj_kernel, 1, [me] + dqs + kvs + weights,
         (sds((TILE, 512), BF16), sds((TILE, 512), F32)),
-        scratch=[pltpu.VMEM((NX, TILE, 256), BF16)] + [pltpu.VMEM((2, TILE, 512), F32)] * 2,
-        flops=536_870_912, nbytes=4_000_000,
+        scratch=[
+            pltpu.VMEM((NX, TILE, 768), BF16), pltpu.VMEM((2, TILE, 512), F32),
+            pltpu.VMEM((2, TILE, 512), F32),
+        ],
+        flops=1_610_612_736, nbytes=8_000_000, mib=16,
     )
     got = gather(send, "head", HEAD_PAIRS)
     got = lax.dynamic_index_in_dim(got, 1 - b, 0, keepdims=False)

time: 189 us -> 202 us (1.069)
  blocking collectives: 80.9 us -> 13.2 us
  waiting for transfers between devices: 40.5 us -> 91.5 us
  starting transfers between devices: 46.6 us -> 73.5 us
  local copies, waits for them, and re-layouts: 0.29 us -> 4.49 us
    all_gather x5 -> x3, blocking collectives: 80.9 us -> 13.2 us  [gather(): return lax.all_gather(array, axis, axis=0, axis_index_groups=groups)]
    ppermute x3 -> x8, waiting for transfers between devices: 0.01 us -> 28.8 us  [the longest x3 18.4 us: step(): w = jnp.concatenate([w, lax.ppermute(w, 'ctx', z_shift(by))])]
    ppermute x3 -> x8, starting transfers between devices: 7.89 us -> 34.9 us  [the longest x3 21.4 us: step(): w = jnp.concatenate([w, lax.ppermute(w, 'ctx', z_shift(by))])]
    ppermute x3, waiting for transfers between devices: 0.01 us -> 18.4 us  [step(): lax.ppermute(dq, 'head', head_shift(-2 * r))]
    ppermute x1, waiting for transfers between devices: 8.89 us -> 15 us  [step(): far_back = lax.ppermute(far, 'ctx', chip_shift(-2))]
    unnamed x23 -> x24, local copies, waits for them, and re-layouts: 0.11 us -> 4.29 us
    pallas_call x3 -> x2, Pallas kernels: 15.1 us -> 13.3 us  [call(): pl.pallas_call(kernel, out_shape=outs, in_specs=[smem] * n_scalar + [vmem...]
  transfers between devices with their start and end apart: 15 -> 20, of which waited for: 5 -> 12; matrix products, arithmetic and copies ran while one was open for 2% -> 1% of each run, Pallas kernels for 5% -> 4%
where the time goes in v1:
time: 202 us; the launch traced here: 199 us
  waiting for transfers between devices  91.5 us (45%)
  starting transfers between devices  73.5 us (36%)
  Pallas kernels  13.3 us (7%)
  blocking collectives  13.2 us (7%)
  local copies, waits for them, and re-layouts  4.49 us (2%)
  other arithmetic  2.58 us (1%)
    ppermute x3, starting transfers between devices, step(): w = jnp.concatenate([w, lax.ppermute(w, 'ctx', z_shift(by))])  21.4 us
    ppermute x3, waiting for transfers between devices, step(): lax.ppermute(dq, 'head', head_shift(-2 * r))  18.4 us
    ppermute x3, waiting for transfers between devices, step(): w = jnp.concatenate([w, lax.ppermute(w, 'ctx', z_shift(by))])  18.4 us
    ppermute x1, waiting for transfers between devices, step(): far_back = lax.ppermute(far, 'ctx', chip_shift(-2))  15 us
    ppermute x1, waiting for transfers between devices, step(): o23 = lax.ppermute(jnp.stack([own, o1]), 'ctx', chip_shift(2))  14.1 us
    ppermute x3, starting transfers between devices, step(): lax.ppermute(dq, 'head', head_shift(-2 * r))  13.4 us
    pallas_call x2, Pallas kernels, call(): pl.pallas_call(kernel, out_shape=outs, in_specs=[smem] * n_scalar + [vmem...  13.3 us
    all_gather x3, blocking collectives, gather(): return lax.all_gather(array, axis, axis=0, axis_index_groups=groups)  13.2 us
  transfers between devices with their start and end apart: 20, of which 12 were waited for; matrix products, arithmetic and copies ran while one was open for 1% of the time, Pallas kernels for 4%

profile of v1, /device:TPU:6, one launch (start us, length us, event | category | flops | bytes accessed | tf_op | source)
XLA Modules:
  0.0 199.3 jit_solution(14397624123390246376)
XLA Ops:
  0.0 6.1 %collective-permute-start.12 = (bf16[64,768]{1,0:T(8,128)(2,1)}, bf16[64,768]{1,0:T(8,128)(2,1)S(1)}, u32[]{:S(2)}, u32[]{:S(2)}) collective-permute-start(bf16[64,768]{1,0:T(8,128)(2,1)} %bitcast.49), channel_id=1, source_target_pairs={{0,0},{1,1},{2,128},{3,129},{4,256},{5,257},{6,384},{7,385},{8,8},... | collective-permute-start | bytes 294920 | tf_op jit(solution)/shard_map/ppermute | solution.py:218
  6.1 7.0 %collective-permute-done.12 = bf16[64,768]{1,0:T(8,128)(2,1)S(1)} collective-permute-done((bf16[64,768]{1,0:T(8,128)(2,1)}, bf16[64,768]{1,0:T(8,128)(2,1)S(1)}, u32[]{:S(2)}, u32[]{:S(2)}) %collective-permute-start.12) | collective-permute-done | bytes 98336 | tf_op jit(solution)/shard_map/ppermute | solution.py:218
  13.1 10.9 %collective-permute-start.13 = (bf16[64,768]{1,0:T(8,128)(2,1)S(1)}, bf16[64,768]{1,0:T(8,128)(2,1)S(1)}, u32[]{:S(2)}, u32[]{:S(2)}) collective-permute-start(bf16[64,768]{1,0:T(8,128)(2,1)S(1)} %collective-permute-done.12), channel_id=1, source_target_pairs={{0,96},{8,104},{16,112},{24,120},{32,0},{40,8},{48,16},{56,24},{64... | collective-permute-start | bytes 294920 | tf_op jit(solution)/shard_map/ppermute | solution.py:220
  24.0 3.7 %collective-permute-done.13 = bf16[64,768]{1,0:T(8,128)(2,1)S(1)} collective-permute-done((bf16[64,768]{1,0:T(8,128)(2,1)S(1)}, bf16[64,768]{1,0:T(8,128)(2,1)S(1)}, u32[]{:S(2)}, u32[]{:S(2)}) %collective-permute-start.13) | collective-permute-done | bytes 98336 | tf_op jit(solution)/shard_map/ppermute | solution.py:220
  27.7 4.8 %collective-permute-start.14 = (bf16[128,768]{1,0:T(8,128)(2,1)S(1)}, bf16[128,768]{1,0:T(8,128)(2,1)S(1)}, u32[]{:S(2)}, u32[]{:S(2)}) collective-permute-start(bf16[128,768]{1,0:T(8,128)(2,1)S(1)} %pad_maximum_fusion.5), channel_id=1, source_target_pairs={{0,64},{8,72},{16,80},{24,88},{32,96},{40,104},{48,112},{56,120},{... | collective-permute-start | bytes 589832 | tf_op jit(solution)/shard_map/ppermute | solution.py:220
  32.5 6.9 %collective-permute-done.14 = bf16[128,768]{1,0:T(8,128)(2,1)S(1)} collective-permute-done((bf16[128,768]{1,0:T(8,128)(2,1)S(1)}, bf16[128,768]{1,0:T(8,128)(2,1)S(1)}, u32[]{:S(2)}, u32[]{:S(2)}) %collective-permute-start.14) | collective-permute-done | bytes 196640 | tf_op jit(solution)/shard_map/ppermute | solution.py:220
  39.4 5.7 %collective-permute-start.15 = (bf16[256,768]{1,0:T(8,128)(2,1)S(1)}, bf16[256,768]{1,0:T(8,128)(2,1)S(1)}, u32[]{:S(2)}, u32[]{:S(2)}) collective-permute-start(bf16[256,768]{1,0:T(8,128)(2,1)S(1)} %pad_maximum_fusion.3), channel_id=1, source_target_pairs={{0,16},{8,24},{16,32},{24,40},{32,48},{40,56},{48,64},{56,72},{64,... | collective-permute-start | bytes 1179656 | tf_op jit(solution)/shard_map/ppermute | solution.py:220
  45.2 7.8 %collective-permute-done.15 = bf16[256,768]{1,0:T(8,128)(2,1)S(1)} collective-permute-done((bf16[256,768]{1,0:T(8,128)(2,1)S(1)}, bf16[256,768]{1,0:T(8,128)(2,1)S(1)}, u32[]{:S(2)}, u32[]{:S(2)}) %collective-permute-start.15) | collective-permute-done | bytes 393248 | tf_op jit(solution)/shard_map/ppermute | solution.py:220
  53.3 2.1 %collective-permute-start.16 = (bf16[512,768]{1,0:T(8,128)(2,1)S(1)}, bf16[512,768]{1,0:T(8,128)(2,1)S(1)}, u32[]{:S(2)}, u32[]{:S(2)}) collective-permute-start(bf16[512,768]{1,0:T(8,128)(2,1)S(1)} %slice_dynamic-update-slice_fusion), channel_id=1, source_target_pairs={{0,8},{8,0},{16,24},{24,16},{32,40},{40,32},{48,56},{56,48},{64,72... | collective-permute-start | bytes 2359304 | tf_op jit(solution)/shard_map/ppermute | solution.py:222
  55.4 2.3 %collective-permute-done.16 = bf16[512,768]{1,0:T(8,128)(2,1)S(1)} collective-permute-done((bf16[512,768]{1,0:T(8,128)(2,1)S(1)}, bf16[512,768]{1,0:T(8,128)(2,1)S(1)}, u32[]{:S(2)}, u32[]{:S(2)}) %collective-permute-start.16) | collective-permute-done | bytes 786464 | tf_op jit(solution)/shard_map/ppermute | solution.py:222
  57.6 0.1 pad_maximum_fusion.own
  57.7 1.9 collective-permute-start.17
  59.7 0.7 fusion.5
  60.4 4.3 %collective-permute-start.1 = (bf16[2,256,128]{2,1,0:T(8,128)(2,1)}, bf16[2,256,128]{2,1,0:T(8,128)(2,1)S(1)}, u32[]{:S(2)}, u32[]{:S(2)}) collective-permute-start(bf16[2,256,128]{2,1,0:T(8,128)(2,1)} %get-tuple-element.18.own), channel_id=1, source_target_pairs={{0,16},{8,24},{16,32},{24,40},{32,48},{40,56},{48,64},{56,72},{64,... | collective-permute-start | bytes 393224 | tf_op jit(solution)/shard_map/ppermute | solution.py:213
  64.7 6.0 %collective-permute-done.1.o1 = bf16[2,256,128]{2,1,0:T(8,128)(2,1)S(1)} collective-permute-done((bf16[2,256,128]{2,1,0:T(8,128)(2,1)}, bf16[2,256,128]{2,1,0:T(8,128)(2,1)S(1)}, u32[]{:S(2)}, u32[]{:S(2)}) %collective-permute-start.1) | collective-permute-done | bytes 131104 | tf_op jit(solution)/shard_map/ppermute | solution.py:213
  70.6 0.7 pad_maximum_fusion.4
  71.4 2.3 %collective-permute-start.2 = (bf16[2,2,256,128]{3,2,1,0:T(8,128)(2,1)}, bf16[2,2,256,128]{3,2,1,0:T(8,128)(2,1)S(1)}, u32[]{:S(2)}, u32[]{:S(2)}) collective-permute-start(bf16[2,2,256,128]{3,2,1,0:T(8,128)(2,1)} %pad_maximum_fusion.4), channel_id=1, source_target_pairs={{0,32},{8,40},{16,48},{24,56},{32,64},{40,72},{48,80},{56,88},{64,... | collective-permute-start | bytes 786440 | tf_op jit(solution)/shard_map/ppermute | solution.py:215
  73.7 1.9 collective-permute-start
  75.7 0.1 stack.45.me
  75.8 14.1 %collective-permute-done.2.o23 = bf16[2,2,256,128]{3,2,1,0:T(8,128)(2,1)S(1)} collective-permute-done((bf16[2,2,256,128]{3,2,1,0:T(8,128)(2,1)}, bf16[2,2,256,128]{3,2,1,0:T(8,128)(2,1)S(1)}, u32[]{:S(2)}, u32[]{:S(2)}) %collective-permute-start.2) | collective-permute-done | bytes 262176 | tf_op jit(solution)/shard_map/ppermute | solution.py:215
  89.9 2.4 %all-gather = bf16[6,2,256,128]{3,2,1,0:T(8,128)(2,1)S(1)} all-gather(bf16[3,2,256,128]{3,2,1,0:T(8,128)(2,1)S(1)} %pad_maximum_fusion.2), channel_id=2, replica_groups={{0,8},{16,24},{32,40},{48,56},{64,72},{80,88},{96,104},{112,120},{128,1..., dimensions={0}, use_global_device_ids=true | all-gather | bytes 1179648 | tf_op jit(solution)/shard_map/all_gather | solution.py:194
  92.3 5.5 %collective-permute-start.19 = (bf16[1024,768]{1,0:T(8,128)(2,1)S(1)}, bf16[1024,768]{1,0:T(8,128)(2,1)}, u32[]{:S(2)}, u32[]{:S(2)}) collective-permute-start(bf16[1024,768]{1,0:T(8,128)(2,1)S(1)} %collective-permute-done.17.near), channel_id=1, source_target_pairs={{0,128},{8,392},{16,144},{24,408},{32,160},{40,424},{48,176},{56,4... | collective-permute-start | bytes 4718600 | tf_op jit(solution)/shard_map/ppermute | solution.py:224
  97.7 1.9 collective-permute-start.18
  99.7 8.9 %shard_map.73 = (bf16[256,512]{1,0:T(8,128)(2,1)S(1)}, f32[4,2,256,128]{3,2,1,0:T(8,128)S(1)}, bf16[2,256,128]{2,1,0:T(8,128)(2,1)S(1)}, bf16[3,2,256,128]{3,2,1,0:T(8,128)(2,1)S(1)}) custom-call(s32[6]{0:T(128)S(1)} %stack.45.me, s32[64]{0:T(128)S(1)} %copy-done.9, bf16[256,512]{1,0:T(8,128)(2,1)S(1)} %copy-done.6, bf16[256,512]{1,0:T(8,128)(2,1)S(1)} %copy-done.7, ...), custom_call_target="tpu_custom_call" | custom-call | flops 2700000000 | bytes 5000000 | tf_op jit(solution)/shard_map/pallas_call | solution.py:178
  108.7 2.5 %all-gather.1 = bf16[6,2,256,128]{3,2,1,0:T(8,128)(2,1)S(1)} all-gather(bf16[3,2,256,128]{3,2,1,0:T(8,128)(2,1)S(1)} %get-tuple-element.13), channel_id=3, replica_groups={{0,8},{16,24},{32,40},{48,56},{64,72},{80,88},{96,104},{112,120},{128,1..., dimensions={0}, use_global_device_ids=true | all-gather | bytes 1179648 | tf_op jit(solution)/shard_map/all_gather | solution.py:194
  111.3 1.9 collective-permute-start.6
  113.2 2.8 %collective-permute-start.8 = (bf16[2,256,128]{2,1,0:T(8,128)(2,1)S(1)}, bf16[2,256,128]{2,1,0:T(8,128)(2,1)S(1)}, u32[]{:S(2)}, u32[]{:S(2)}) collective-permute-start(bf16[2,256,128]{2,1,0:T(8,128)(2,1)S(1)} %get-tuple-element.14), channel_id=1, source_target_pairs={{8,0},{24,16},{40,32},{56,48},{72,64},{88,80},{104,96},{120,112},{... | collective-permute-start | bytes 393224 | tf_op jit(solution)/shard_map/ppermute | solution.py:244
  116.0 15.0 %collective-permute-done.6 = bf16[2,2,256,128]{3,2,1,0:T(8,128)(2,1)S(1)} collective-permute-done((bf16[2,2,256,128]{3,2,1,0:T(8,128)(2,1)S(1)}, bf16[2,2,256,128]{3,2,1,0:T(8,128)(2,1)S(1)}, u32[]{:S(2)}, u32[]{:S(2)}) %collective-permute-start.6) | collective-permute-done | bytes 262176 | tf_op jit(solution)/shard_map/ppermute | solution.py:243
  131.0 1.9 collective-permute-start.7
  132.9 3.8 %collective-permute-start.5 = (bf16[256,512]{1,0:T(8,128)(2,1)S(1)}, bf16[256,512]{1,0:T(8,128)(2,1)S(1)}, u32[]{:S(2)}, u32[]{:S(2)}) collective-permute-start(bf16[256,512]{1,0:T(8,128)(2,1)S(1)} %get-tuple-element.11.d0), channel_id=1, source_target_pairs={{0,2},{1,3},{2,4},{3,5},{4,6},{5,7},{6,0},{7,1},{8,10},{9,11},{10,... | collective-permute-start | bytes 786440 | tf_op jit(solution)/shard_map/ppermute | solution.py:251
  136.7 7.3 %collective-permute-start.4 = (bf16[256,512]{1,0:T(8,128)(2,1)S(1)}, bf16[256,512]{1,0:T(8,128)(2,1)S(1)}, u32[]{:S(2)}, u32[]{:S(2)}) collective-permute-start(bf16[256,512]{1,0:T(8,128)(2,1)S(1)} %get-tuple-element.11.d0), channel_id=1, source_target_pairs={{0,4},{1,5},{2,6},{3,7},{4,0},{5,1},{6,2},{7,3},{8,12},{9,13},{10,... | collective-permute-start | bytes 786440 | tf_op jit(solution)/shard_map/ppermute | solution.py:251
  144.0 2.4 %collective-permute-start.3 = (bf16[256,512]{1,0:T(8,128)(2,1)S(1)}, bf16[256,512]{1,0:T(8,128)(2,1)S(1)}, u32[]{:S(2)}, u32[]{:S(2)}) collective-permute-start(bf16[256,512]{1,0:T(8,128)(2,1)S(1)} %get-tuple-element.11.d0), channel_id=1, source_target_pairs={{0,6},{1,7},{2,0},{3,1},{4,2},{5,3},{6,4},{7,5},{8,14},{9,15},{10,... | collective-permute-start | bytes 786440 | tf_op jit(solution)/shard_map/ppermute | solution.py:251
  146.4 0.1 fusion.4.k0
  146.5 3.3 %collective-permute-done.5.d3 = bf16[256,512]{1,0:T(8,128)(2,1)S(1)} collective-permute-done((bf16[256,512]{1,0:T(8,128)(2,1)S(1)}, bf16[256,512]{1,0:T(8,128)(2,1)S(1)}, u32[]{:S(2)}, u32[]{:S(2)}) %collective-permute-start.5) | collective-permute-done | bytes 262176 | tf_op jit(solution)/shard_map/ppermute | solution.py:251
  149.8 2.3 %collective-permute-start.11 = (bf16[2,256,128]{2,1,0:T(8,128)(2,1)S(1)}, bf16[2,256,128]{2,1,0:T(8,128)(2,1)}, u32[]{:S(2)}, u32[]{:S(2)}) collective-permute-start(bf16[2,256,128]{2,1,0:T(8,128)(2,1)S(1)} %fusion.4.k0), channel_id=1, source_target_pairs={{0,2},{1,3},{2,4},{3,5},{4,6},{5,7},{6,0},{7,1},{8,10},{9,11},{10,... | collective-permute-start | bytes 393224 | tf_op jit(solution)/shard_map/ppermute | solution.py:252
  152.1 15.1 %collective-permute-done.4.d2 = bf16[256,512]{1,0:T(8,128)(2,1)S(1)} collective-permute-done((bf16[256,512]{1,0:T(8,128)(2,1)S(1)}, bf16[256,512]{1,0:T(8,128)(2,1)S(1)}, u32[]{:S(2)}, u32[]{:S(2)}) %collective-permute-start.4) | collective-permute-done | bytes 262176 | tf_op jit(solution)/shard_map/ppermute | solution.py:251
  167.2 0.7 copy-done.2
  167.9 1.9 collective-permute-start.10
  169.9 0.7 copy-done.4
  170.6 1.9 collective-permute-start.9
  172.5 6.3 %collective-permute-done.10.k2 = bf16[2,256,128]{2,1,0:T(8,128)(2,1)} collective-permute-done((bf16[2,256,128]{2,1,0:T(8,128)(2,1)S(1)}, bf16[2,256,128]{2,1,0:T(8,128)(2,1)}, u32[]{:S(2)}, u32[]{:S(2)}) %collective-permute-start.10) | collective-permute-done | bytes 131104 | tf_op jit(solution)/shard_map/ppermute | solution.py:252
  178.8 4.1 %collective-permute-done.9.k1 = bf16[2,256,128]{2,1,0:T(8,128)(2,1)} collective-permute-done((bf16[2,256,128]{2,1,0:T(8,128)(2,1)S(1)}, bf16[2,256,128]{2,1,0:T(8,128)(2,1)}, u32[]{:S(2)}, u32[]{:S(2)}) %collective-permute-start.9) | collective-permute-done | bytes 131104 | tf_op jit(solution)/shard_map/ppermute | solution.py:252
  182.9 0.9 copy-done.1
  183.9 0.9 copy-done.3
  184.8 0.9 copy-done.5
  185.8 4.4 %shard_map.74 = (bf16[256,512]{1,0:T(8,128)(2,1)S(1)}, f32[256,512]{1,0:T(8,128)S(1)}) custom-call(s32[6]{0:T(128)S(1)} %stack.45.me, bf16[256,512]{1,0:T(8,128)(2,1)S(1)} %copy-done.1, bf16[256,512]{1,0:T(8,128)(2,1)S(1)} %copy-done.5, bf16[256,512]{1,0:T(8,128)(2,1)S(1)} %copy-done.3, bf16[256,512]{1,0:T(8,128)(2,1)S(1)} %collective-permute-done.5.d3, ...), custom_call_target="tpu_custom_call" | custom-call | flops 1610612736 | bytes 8000000 | tf_op jit(solution)/shard_map/pallas_call | solution.py:178
  190.2 8.3 %all-gather.2 = bf16[512,512]{1,0:T(8,128)(2,1)S(1)} all-gather(bf16[256,512]{1,0:T(8,128)(2,1)S(1)} %get-tuple-element.16), channel_id=4, replica_groups={{0,1},{2,3},{4,5},{6,7},{8,9},{10,11},{12,13},{14,15},{16,17},{18,19},{..., dimensions={0}, use_global_device_ids=true | all-gather | bytes 786432 | tf_op jit(solution)/shard_map/all_gather | solution.py:194
  198.5 0.8 fusion
  (41 shorter events, 0.4 us)
Async XLA Ops:
  0.0 13.1 %collective-permute-start.12 = (bf16[64,768]{1,0:T(8,128)(2,1)}, bf16[64,768]{1,0:T(8,128)(2,1)S(1)}, u32[]{:S(2)}, u32[]{:S(2)}) collective-permute-start(bf16[64,768]{1,0:T(8,128)(2,1)} %bitcast.49), channel_id=1, source_target_pairs={{0,0},{1,1},{2,128},{3,129},{4,256},{5,257},{6,384},{7,385},{8,8},... | collective-permute-start | bytes 294920 | tf_op jit(solution)/shard_map/ppermute | solution.py:218
  13.1 14.6 %collective-permute-start.13 = (bf16[64,768]{1,0:T(8,128)(2,1)S(1)}, bf16[64,768]{1,0:T(8,128)(2,1)S(1)}, u32[]{:S(2)}, u32[]{:S(2)}) collective-permute-start(bf16[64,768]{1,0:T(8,128)(2,1)S(1)} %collective-permute-done.12), channel_id=1, source_target_pairs={{0,96},{8,104},{16,112},{24,120},{32,0},{40,8},{48,16},{56,24},{64... | collective-permute-start | bytes 294920 | tf_op jit(solution)/shard_map/ppermute | solution.py:220
  27.7 11.6 %collective-permute-start.14 = (bf16[128,768]{1,0:T(8,128)(2,1)S(1)}, bf16[128,768]{1,0:T(8,128)(2,1)S(1)}, u32[]{:S(2)}, u32[]{:S(2)}) collective-permute-start(bf16[128,768]{1,0:T(8,128)(2,1)S(1)} %pad_maximum_fusion.5), channel_id=1, source_target_pairs={{0,64},{8,72},{16,80},{24,88},{32,96},{40,104},{48,112},{56,120},{... | collective-permute-start | bytes 589832 | tf_op jit(solution)/shard_map/ppermute | solution.py:220
  39.4 13.7 %collective-permute-start.15 = (bf16[256,768]{1,0:T(8,128)(2,1)S(1)}, bf16[256,768]{1,0:T(8,128)(2,1)S(1)}, u32[]{:S(2)}, u32[]{:S(2)}) collective-permute-start(bf16[256,768]{1,0:T(8,128)(2,1)S(1)} %pad_maximum_fusion.3), channel_id=1, source_target_pairs={{0,16},{8,24},{16,32},{24,40},{32,48},{40,56},{48,64},{56,72},{64,... | collective-permute-start | bytes 1179656 | tf_op jit(solution)/shard_map/ppermute | solution.py:220
  53.3 6.4 %copy-start.10 = (bf16[256,128]{1,0:T(8,128)(2,1)S(1)}, bf16[256,128]{1,0:T(8,128)(2,1)}, u32[]{:S(2)}) copy-start(bf16[256,128]{1,0:T(8,128)(2,1)} %param.9) | copy-start | bytes 196612
  53.3 6.4 %copy-start.11 = (bf16[256,128]{1,0:T(8,128)(2,1)S(1)}, bf16[256,128]{1,0:T(8,128)(2,1)}, u32[]{:S(2)}) copy-start(bf16[256,128]{1,0:T(8,128)(2,1)} %param.8) | copy-start | bytes 196612
  53.3 4.3 %collective-permute-start.16 = (bf16[512,768]{1,0:T(8,128)(2,1)S(1)}, bf16[512,768]{1,0:T(8,128)(2,1)S(1)}, u32[]{:S(2)}, u32[]{:S(2)}) collective-permute-start(bf16[512,768]{1,0:T(8,128)(2,1)S(1)} %slice_dynamic-update-slice_fusion), channel_id=1, source_target_pairs={{0,8},{8,0},{16,24},{24,16},{32,40},{40,32},{48,56},{56,48},{64,72... | collective-permute-start | bytes 2359304 | tf_op jit(solution)/shard_map/ppermute | solution.py:222
  57.7 42.0 %copy-start.9 = (s32[64]{0:T(128)S(1)}, s32[64]{0:T(128)}, u32[]{:S(2)}) copy-start(s32[64]{0:T(128)} %lengths.1) | copy-start | bytes 772
  57.7 34.5 %collective-permute-start.17 = (bf16[1024,768]{1,0:T(8,128)(2,1)S(1)}, bf16[1024,768]{1,0:T(8,128)(2,1)S(1)}, u32[]{:S(2)}, u32[]{:S(2)}) collective-permute-start(bf16[1024,768]{1,0:T(8,128)(2,1)S(1)} %pad_maximum_fusion.own), channel_id=1, source_target_pairs={{0,128},{8,392},{16,144},{24,408},{32,160},{40,424},{48,176},{56,4... | collective-permute-start | bytes 4718600 | tf_op jit(solution)/shard_map/ppermute | solution.py:223
  60.4 10.3 %collective-permute-start.1 = (bf16[2,256,128]{2,1,0:T(8,128)(2,1)}, bf16[2,256,128]{2,1,0:T(8,128)(2,1)S(1)}, u32[]{:S(2)}, u32[]{:S(2)}) collective-permute-start(bf16[2,256,128]{2,1,0:T(8,128)(2,1)} %get-tuple-element.18.own), channel_id=1, source_target_pairs={{0,16},{8,24},{16,32},{24,40},{32,48},{40,56},{48,64},{56,72},{64,... | collective-permute-start | bytes 393224 | tf_op jit(solution)/shard_map/ppermute | solution.py:213
  71.4 18.5 %collective-permute-start.2 = (bf16[2,2,256,128]{3,2,1,0:T(8,128)(2,1)}, bf16[2,2,256,128]{3,2,1,0:T(8,128)(2,1)S(1)}, u32[]{:S(2)}, u32[]{:S(2)}) collective-permute-start(bf16[2,2,256,128]{3,2,1,0:T(8,128)(2,1)} %pad_maximum_fusion.4), channel_id=1, source_target_pairs={{0,32},{8,40},{16,48},{24,56},{32,64},{40,72},{48,80},{56,88},{64,... | collective-permute-start | bytes 786440 | tf_op jit(solution)/shard_map/ppermute | solution.py:215
  73.7 26.0 %collective-permute-start = (bf16[2,256,128]{2,1,0:T(8,128)(2,1)}, bf16[2,256,128]{2,1,0:T(8,128)(2,1)}, u32[]{:S(2)}, u32[]{:S(2)}) collective-permute-start(bf16[2,256,128]{2,1,0:T(8,128)(2,1)} %get-tuple-element.18.own), channel_id=1, source_target_pairs={{0,8},{16,24},{32,40},{48,56},{64,72},{80,88},{96,104},{112,120},{... | collective-permute-start | bytes 393224 | tf_op jit(solution)/shard_map/ppermute | solution.py:214
  75.7 24.0 %copy-start.6 = (bf16[256,512]{1,0:T(8,128)(2,1)S(1)}, bf16[256,512]{1,0:T(8,128)(2,1)}, u32[]{:S(2)}) copy-start(bf16[256,512]{1,0:T(8,128)(2,1)} %q_ref.1) | copy-start | bytes 786436
  75.7 24.0 %copy-start.7 = (bf16[256,512]{1,0:T(8,128)(2,1)S(1)}, bf16[256,512]{1,0:T(8,128)(2,1)}, u32[]{:S(2)}) copy-start(bf16[256,512]{1,0:T(8,128)(2,1)} %do_ref.1) | copy-start | bytes 786436
  75.8 24.0 %copy-start.8 = (bf16[256,512]{1,0:T(8,128)(2,1)S(1)}, bf16[256,512]{1,0:T(8,128)(2,1)}, u32[]{:S(2)}) copy-start(bf16[256,512]{1,0:T(8,128)(2,1)} %out_ref.1) | copy-start | bytes 786436
  92.3 90.7 %collective-permute-start.19 = (bf16[1024,768]{1,0:T(8,128)(2,1)S(1)}, bf16[1024,768]{1,0:T(8,128)(2,1)}, u32[]{:S(2)}, u32[]{:S(2)}) collective-permute-start(bf16[1024,768]{1,0:T(8,128)(2,1)S(1)} %collective-permute-done.17.near), channel_id=1, source_target_pairs={{0,128},{8,392},{16,144},{24,408},{32,160},{40,424},{48,176},{56,4... | collective-permute-start | bytes 4718600 | tf_op jit(solution)/shard_map/ppermute | solution.py:224
  97.7 85.2 %collective-permute-start.18 = (bf16[1024,768]{1,0:T(8,128)(2,1)S(1)}, bf16[1024,768]{1,0:T(8,128)(2,1)}, u32[]{:S(2)}, u32[]{:S(2)}) collective-permute-start(bf16[1024,768]{1,0:T(8,128)(2,1)S(1)} %collective-permute-done.17.near), channel_id=1, source_target_pairs={{0,8},{8,0},{16,24},{24,16},{32,40},{40,32},{48,56},{56,48},{64,72... | collective-permute-start | bytes 4718600 | tf_op jit(solution)/shard_map/ppermute | solution.py:225
  108.7 37.8 %copy-start = (bf16[256,512]{1,0:T(8,128)(2,1)}, bf16[256,512]{1,0:T(8,128)(2,1)S(1)}, u32[]{:S(2)}) copy-start(bf16[256,512]{1,0:T(8,128)(2,1)S(1)} %get-tuple-element.11.d0) | copy-start | bytes 786436
  111.3 19.7 %collective-permute-start.6 = (bf16[2,2,256,128]{3,2,1,0:T(8,128)(2,1)S(1)}, bf16[2,2,256,128]{3,2,1,0:T(8,128)(2,1)S(1)}, u32[]{:S(2)}, u32[]{:S(2)}) collective-permute-start(bf16[2,2,256,128]{3,2,1,0:T(8,128)(2,1)S(1)} %fusion.1), channel_id=1, source_target_pairs={{0,480},{8,488},{16,496},{24,504},{32,0},{40,8},{48,16},{56,24},{6... | collective-permute-start | bytes 786440 | tf_op jit(solution)/shard_map/ppermute | solution.py:243
  113.2 23.5 %collective-permute-start.8 = (bf16[2,256,128]{2,1,0:T(8,128)(2,1)S(1)}, bf16[2,256,128]{2,1,0:T(8,128)(2,1)S(1)}, u32[]{:S(2)}, u32[]{:S(2)}) collective-permute-start(bf16[2,256,128]{2,1,0:T(8,128)(2,1)S(1)} %get-tuple-element.14), channel_id=1, source_target_pairs={{8,0},{24,16},{40,32},{56,48},{72,64},{88,80},{104,96},{120,112},{... | collective-permute-start | bytes 393224 | tf_op jit(solution)/shard_map/ppermute | solution.py:244
  131.0 13.0 %collective-permute-start.7 = (bf16[2,256,128]{2,1,0:T(8,128)(2,1)S(1)}, bf16[2,256,128]{2,1,0:T(8,128)(2,1)S(1)}, u32[]{:S(2)}, u32[]{:S(2)}) collective-permute-start(bf16[2,256,128]{2,1,0:T(8,128)(2,1)S(1)} %fusion.2), channel_id=1, source_target_pairs={{0,496},{8,504},{16,0},{24,8},{32,16},{40,24},{48,32},{56,40},{64,... | collective-permute-start | bytes 393224 | tf_op jit(solution)/shard_map/ppermute | solution.py:246
  132.9 16.8 %collective-permute-start.5 = (bf16[256,512]{1,0:T(8,128)(2,1)S(1)}, bf16[256,512]{1,0:T(8,128)(2,1)S(1)}, u32[]{:S(2)}, u32[]{:S(2)}) collective-permute-start(bf16[256,512]{1,0:T(8,128)(2,1)S(1)} %get-tuple-element.11.d0), channel_id=1, source_target_pairs={{0,2},{1,3},{2,4},{3,5},{4,6},{5,7},{6,0},{7,1},{8,10},{9,11},{10,... | collective-permute-start | bytes 786440 | tf_op jit(solution)/shard_map/ppermute | solution.py:251
  136.7 30.5 %collective-permute-start.4 = (bf16[256,512]{1,0:T(8,128)(2,1)S(1)}, bf16[256,512]{1,0:T(8,128)(2,1)S(1)}, u32[]{:S(2)}, u32[]{:S(2)}) collective-permute-start(bf16[256,512]{1,0:T(8,128)(2,1)S(1)} %get-tuple-element.11.d0), channel_id=1, source_target_pairs={{0,4},{1,5},{2,6},{3,7},{4,0},{5,1},{6,2},{7,3},{8,12},{9,13},{10,... | collective-permute-start | bytes 786440 | tf_op jit(solution)/shard_map/ppermute | solution.py:251
  144.0 25.8 %collective-permute-start.3 = (bf16[256,512]{1,0:T(8,128)(2,1)S(1)}, bf16[256,512]{1,0:T(8,128)(2,1)S(1)}, u32[]{:S(2)}, u32[]{:S(2)}) collective-permute-start(bf16[256,512]{1,0:T(8,128)(2,1)S(1)} %get-tuple-element.11.d0), channel_id=1, source_target_pairs={{0,6},{1,7},{2,0},{3,1},{4,2},{5,3},{6,4},{7,5},{8,14},{9,15},{10,... | collective-permute-start | bytes 786440 | tf_op jit(solution)/shard_map/ppermute | solution.py:251
  149.8 22.7 %collective-permute-start.11 = (bf16[2,256,128]{2,1,0:T(8,128)(2,1)S(1)}, bf16[2,256,128]{2,1,0:T(8,128)(2,1)}, u32[]{:S(2)}, u32[]{:S(2)}) collective-permute-start(bf16[2,256,128]{2,1,0:T(8,128)(2,1)S(1)} %fusion.4.k0), channel_id=1, source_target_pairs={{0,2},{1,3},{2,4},{3,5},{4,6},{5,7},{6,0},{7,1},{8,10},{9,11},{10,... | collective-permute-start | bytes 393224 | tf_op jit(solution)/shard_map/ppermute | solution.py:252
  167.2 0.7 copy-start.2
  167.9 10.9 %collective-permute-start.10 = (bf16[2,256,128]{2,1,0:T(8,128)(2,1)S(1)}, bf16[2,256,128]{2,1,0:T(8,128)(2,1)}, u32[]{:S(2)}, u32[]{:S(2)}) collective-permute-start(bf16[2,256,128]{2,1,0:T(8,128)(2,1)S(1)} %fusion.4.k0), channel_id=1, source_target_pairs={{0,4},{1,5},{2,6},{3,7},{4,0},{5,1},{6,2},{7,3},{8,12},{9,13},{10,... | collective-permute-start | bytes 393224 | tf_op jit(solution)/shard_map/ppermute | solution.py:252
  169.9 0.7 copy-start.4
  170.6 12.3 %collective-permute-start.9 = (bf16[2,256,128]{2,1,0:T(8,128)(2,1)S(1)}, bf16[2,256,128]{2,1,0:T(8,128)(2,1)}, u32[]{:S(2)}, u32[]{:S(2)}) collective-permute-start(bf16[2,256,128]{2,1,0:T(8,128)(2,1)S(1)} %fusion.4.k0), channel_id=1, source_target_pairs={{0,6},{1,7},{2,0},{3,1},{4,2},{5,3},{6,4},{7,5},{8,14},{9,15},{10,... | collective-permute-start | bytes 393224 | tf_op jit(solution)/shard_map/ppermute | solution.py:252
  182.9 1.0 copy-start.1
  183.9 0.9 copy-start.3
  184.8 0.9 copy-start.5

commit v2 on v1

--- a/solution.py
+++ b/solution.py
@@ -144,7 +144,7 @@
 
 
 def proj_kernel(
-    me, d0, d1, d2, d3, k0, k1, k2, k3, own, near, other, last,
+    me, d0, d1, d2, d3, k0, k1, k2, k3, own, near, other, half, rest,
     send_ref, keep_ref, heads, acc_ref, full,
 ):
     x, core, k, b = me[1], me[3], me[4], me[5]
@@ -156,10 +156,10 @@
     up = 1 - 2 * core
     here, behind, ahead = heads[x], heads[(x - up + NX) % NX], heads[(x + up + NX) % NX]
     far = heads[(x + 2) % NX]
-    for side, rows, swapped in ((0, FIRST, SECOND), (1, SECOND, FIRST)):
+    for side, rows, swapped, last in ((0, FIRST, SECOND, half), (1, SECOND, FIRST, rest)):
         acc_ref[side] = (
             dot(here, own[rows, :], NT) + dot(behind, near[rows, :], NT)
-            + dot(ahead, other[swapped, :], NT) + dot(far, last[rows, :], NT)
+            + dot(ahead, other[swapped, :], NT) + dot(far, last[...], NT)
         )
     left = lax.broadcasted_iota(jnp.int32, (TILE, 128), 1) < 64
     for n in range(4):
@@ -221,8 +221,8 @@
     w = in_order(w, chip % NZ)
     w = jnp.concatenate([w, lax.ppermute(w, "ctx", CORE_SWAP)])
     w1 = lax.ppermute(w, "ctx", X_SPLIT)
-    w2 = lax.ppermute(w1, "ctx", X_SPLIT)
-    weights = [w, w1, lax.ppermute(w1, "ctx", CORE_SWAP), w2]
+    w2 = lax.ppermute(w1[:512], "ctx", X_SPLIT)
+    weights = [w, w1, lax.ppermute(w1, "ctx", CORE_SWAP), w2, lax.ppermute(w2, "ctx", CORE_SWAP)]
 
     dq, g_own, g_last, g_x = call(
         attention_kernel, 2,

time: 202 us -> 202 us (level)
  waiting for transfers between devices: 91.5 us -> 88.7 us
  starting transfers between devices: 73.5 us -> 76.1 us
    ppermute x1, waiting for transfers between devices: 15 us -> 12.4 us  [step(): far_back = lax.ppermute(far, 'ctx', chip_shift(-2))]
    ppermute x2 -> x3, starting transfers between devices: 7.38 us -> 9.66 us  [the longest x1 5.45 us: step(): w2 = lax.ppermute(w1[:512], 'ctx', X_SPLIT)]
  transfers between devices with their start and end apart: 20 -> 21, of which waited for: 12 -> 12; matrix products, arithmetic and copies ran while one was open for 1% -> 1% of each run, Pallas kernels for 4% -> 4%
where the time goes in v2:
time: 202 us; the launch traced here: 200 us
  waiting for transfers between devices  88.7 us (44%)
  starting transfers between devices  76.1 us (38%)
  blocking collectives  13.6 us (7%)
  Pallas kernels  13.3 us (7%)
  local copies, waits for them, and re-layouts  4.54 us (2%)
  other arithmetic  2.57 us (1%)
    ppermute x3, starting transfers between devices, step(): w = jnp.concatenate([w, lax.ppermute(w, 'ctx', z_shift(by))])  21.4 us
    ppermute x3, waiting for transfers between devices, step(): w = jnp.concatenate([w, lax.ppermute(w, 'ctx', z_shift(by))])  18.4 us
    ppermute x3, waiting for transfers between devices, step(): lax.ppermute(dq, 'head', head_shift(-2 * r))  18.3 us
    ppermute x1, waiting for transfers between devices, step(): o23 = lax.ppermute(jnp.stack([own, o1]), 'ctx', chip_shift(2))  14.1 us
    all_gather x3, blocking collectives, gather(): return lax.all_gather(array, axis, axis=0, axis_index_groups=groups)  13.6 us
    ppermute x3, starting transfers between devices, step(): lax.ppermute(dq, 'head', head_shift(-2 * r))  13.5 us
    pallas_call x2, Pallas kernels, call(): pl.pallas_call(kernel, out_shape=outs, in_specs=[smem] * n_scalar + [vmem...  13.3 us
    ppermute x1, waiting for transfers between devices, step(): far_back = lax.ppermute(far, 'ctx', chip_shift(-2))  12.4 us
  transfers between devices with their start and end apart: 21, of which 12 were waited for; matrix products, arithmetic and copies ran while one was open for 1% of the time, Pallas kernels for 4%

profile of v2, /device:TPU:6, one launch (start us, length us, event | category | flops | bytes accessed | tf_op | source)
XLA Modules:
  0.0 199.5 jit_solution(2248528179643259853)
XLA Ops:
  0.0 6.1 %collective-permute-start.12 = (bf16[64,768]{1,0:T(8,128)(2,1)}, bf16[64,768]{1,0:T(8,128)(2,1)S(1)}, u32[]{:S(2)}, u32[]{:S(2)}) collective-permute-start(bf16[64,768]{1,0:T(8,128)(2,1)} %bitcast.49), channel_id=1, source_target_pairs={{0,0},{1,1},{2,128},{3,129},{4,256},{5,257},{6,384},{7,385},{8,8},... | collective-permute-start | bytes 294920 | tf_op jit(solution)/shard_map/ppermute | solution.py:218
  6.1 7.0 %collective-permute-done.12 = bf16[64,768]{1,0:T(8,128)(2,1)S(1)} collective-permute-done((bf16[64,768]{1,0:T(8,128)(2,1)}, bf16[64,768]{1,0:T(8,128)(2,1)S(1)}, u32[]{:S(2)}, u32[]{:S(2)}) %collective-permute-start.12) | collective-permute-done | bytes 98336 | tf_op jit(solution)/shard_map/ppermute | solution.py:218
  13.1 10.9 %collective-permute-start.13 = (bf16[64,768]{1,0:T(8,128)(2,1)S(1)}, bf16[64,768]{1,0:T(8,128)(2,1)S(1)}, u32[]{:S(2)}, u32[]{:S(2)}) collective-permute-start(bf16[64,768]{1,0:T(8,128)(2,1)S(1)} %collective-permute-done.12), channel_id=1, source_target_pairs={{0,96},{8,104},{16,112},{24,120},{32,0},{40,8},{48,16},{56,24},{64... | collective-permute-start | bytes 294920 | tf_op jit(solution)/shard_map/ppermute | solution.py:220
  24.0 3.7 %collective-permute-done.13 = bf16[64,768]{1,0:T(8,128)(2,1)S(1)} collective-permute-done((bf16[64,768]{1,0:T(8,128)(2,1)S(1)}, bf16[64,768]{1,0:T(8,128)(2,1)S(1)}, u32[]{:S(2)}, u32[]{:S(2)}) %collective-permute-start.13) | collective-permute-done | bytes 98336 | tf_op jit(solution)/shard_map/ppermute | solution.py:220
  27.7 4.8 %collective-permute-start.14 = (bf16[128,768]{1,0:T(8,128)(2,1)S(1)}, bf16[128,768]{1,0:T(8,128)(2,1)S(1)}, u32[]{:S(2)}, u32[]{:S(2)}) collective-permute-start(bf16[128,768]{1,0:T(8,128)(2,1)S(1)} %pad_maximum_fusion.5), channel_id=1, source_target_pairs={{0,64},{8,72},{16,80},{24,88},{32,96},{40,104},{48,112},{56,120},{... | collective-permute-start | bytes 589832 | tf_op jit(solution)/shard_map/ppermute | solution.py:220
  32.5 6.9 %collective-permute-done.14 = bf16[128,768]{1,0:T(8,128)(2,1)S(1)} collective-permute-done((bf16[128,768]{1,0:T(8,128)(2,1)S(1)}, bf16[128,768]{1,0:T(8,128)(2,1)S(1)}, u32[]{:S(2)}, u32[]{:S(2)}) %collective-permute-start.14) | collective-permute-done | bytes 196640 | tf_op jit(solution)/shard_map/ppermute | solution.py:220
  39.4 5.7 %collective-permute-start.15 = (bf16[256,768]{1,0:T(8,128)(2,1)S(1)}, bf16[256,768]{1,0:T(8,128)(2,1)S(1)}, u32[]{:S(2)}, u32[]{:S(2)}) collective-permute-start(bf16[256,768]{1,0:T(8,128)(2,1)S(1)} %pad_maximum_fusion.3), channel_id=1, source_target_pairs={{0,16},{8,24},{16,32},{24,40},{32,48},{40,56},{48,64},{56,72},{64,... | collective-permute-start | bytes 1179656 | tf_op jit(solution)/shard_map/ppermute | solution.py:220
  45.2 7.8 %collective-permute-done.15 = bf16[256,768]{1,0:T(8,128)(2,1)S(1)} collective-permute-done((bf16[256,768]{1,0:T(8,128)(2,1)S(1)}, bf16[256,768]{1,0:T(8,128)(2,1)S(1)}, u32[]{:S(2)}, u32[]{:S(2)}) %collective-permute-start.15) | collective-permute-done | bytes 393248 | tf_op jit(solution)/shard_map/ppermute | solution.py:220
  53.3 2.1 %collective-permute-start.16 = (bf16[512,768]{1,0:T(8,128)(2,1)S(1)}, bf16[512,768]{1,0:T(8,128)(2,1)S(1)}, u32[]{:S(2)}, u32[]{:S(2)}) collective-permute-start(bf16[512,768]{1,0:T(8,128)(2,1)S(1)} %slice_dynamic-update-slice_fusion), channel_id=1, source_target_pairs={{0,8},{8,0},{16,24},{24,16},{32,40},{40,32},{48,56},{56,48},{64,72... | collective-permute-start | bytes 2359304 | tf_op jit(solution)/shard_map/ppermute | solution.py:222
  55.4 2.3 %collective-permute-done.16 = bf16[512,768]{1,0:T(8,128)(2,1)S(1)} collective-permute-done((bf16[512,768]{1,0:T(8,128)(2,1)S(1)}, bf16[512,768]{1,0:T(8,128)(2,1)S(1)}, u32[]{:S(2)}, u32[]{:S(2)}) %collective-permute-start.16) | collective-permute-done | bytes 786464 | tf_op jit(solution)/shard_map/ppermute | solution.py:222
  57.6 0.1 pad_maximum_fusion.own
  57.7 1.9 collective-permute-start.17
  59.7 0.7 fusion.5
  60.4 4.3 %collective-permute-start.1 = (bf16[2,256,128]{2,1,0:T(8,128)(2,1)}, bf16[2,256,128]{2,1,0:T(8,128)(2,1)S(1)}, u32[]{:S(2)}, u32[]{:S(2)}) collective-permute-start(bf16[2,256,128]{2,1,0:T(8,128)(2,1)} %get-tuple-element.18.own), channel_id=1, source_target_pairs={{0,16},{8,24},{16,32},{24,40},{32,48},{40,56},{48,64},{56,72},{64,... | collective-permute-start | bytes 393224 | tf_op jit(solution)/shard_map/ppermute | solution.py:213
  64.7 6.0 %collective-permute-done.1.o1 = bf16[2,256,128]{2,1,0:T(8,128)(2,1)S(1)} collective-permute-done((bf16[2,256,128]{2,1,0:T(8,128)(2,1)}, bf16[2,256,128]{2,1,0:T(8,128)(2,1)S(1)}, u32[]{:S(2)}, u32[]{:S(2)}) %collective-permute-start.1) | collective-permute-done | bytes 131104 | tf_op jit(solution)/shard_map/ppermute | solution.py:213
  70.6 0.7 pad_maximum_fusion.4
  71.4 2.3 %collective-permute-start.2 = (bf16[2,2,256,128]{3,2,1,0:T(8,128)(2,1)}, bf16[2,2,256,128]{3,2,1,0:T(8,128)(2,1)S(1)}, u32[]{:S(2)}, u32[]{:S(2)}) collective-permute-start(bf16[2,2,256,128]{3,2,1,0:T(8,128)(2,1)} %pad_maximum_fusion.4), channel_id=1, source_target_pairs={{0,32},{8,40},{16,48},{24,56},{32,64},{40,72},{48,80},{56,88},{64,... | collective-permute-start | bytes 786440 | tf_op jit(solution)/shard_map/ppermute | solution.py:215
  73.7 1.9 collective-permute-start
  75.6 0.1 stack.45.me
  75.7 14.1 %collective-permute-done.2.o23 = bf16[2,2,256,128]{3,2,1,0:T(8,128)(2,1)S(1)} collective-permute-done((bf16[2,2,256,128]{3,2,1,0:T(8,128)(2,1)}, bf16[2,2,256,128]{3,2,1,0:T(8,128)(2,1)S(1)}, u32[]{:S(2)}, u32[]{:S(2)}) %collective-permute-start.2) | collective-permute-done | bytes 262176 | tf_op jit(solution)/shard_map/ppermute | solution.py:215
  89.9 2.5 %all-gather = bf16[6,2,256,128]{3,2,1,0:T(8,128)(2,1)S(1)} all-gather(bf16[3,2,256,128]{3,2,1,0:T(8,128)(2,1)S(1)} %pad_maximum_fusion.2), channel_id=2, replica_groups={{0,8},{16,24},{32,40},{48,56},{64,72},{80,88},{96,104},{112,120},{128,1..., dimensions={0}, use_global_device_ids=true | all-gather | bytes 1179648 | tf_op jit(solution)/shard_map/all_gather | solution.py:194
  92.5 5.5 %collective-permute-start.19 = (bf16[512,768]{1,0:T(8,128)(2,1)S(1)}, bf16[512,768]{1,0:T(8,128)(2,1)}, u32[]{:S(2)}, u32[]{:S(2)}) collective-permute-start(bf16[512,768]{1,0:T(8,128)(2,1)S(1)} %slice.66), channel_id=1, source_target_pairs={{0,128},{8,392},{16,144},{24,408},{32,160},{40,424},{48,176},{56,4... | collective-permute-start | bytes 2359304 | tf_op jit(solution)/shard_map/ppermute | solution.py:224
  98.0 1.9 collective-permute-start.18
  99.9 8.9 %shard_map.73 = (bf16[256,512]{1,0:T(8,128)(2,1)S(1)}, f32[4,2,256,128]{3,2,1,0:T(8,128)S(1)}, bf16[2,256,128]{2,1,0:T(8,128)(2,1)S(1)}, bf16[3,2,256,128]{3,2,1,0:T(8,128)(2,1)S(1)}) custom-call(s32[6]{0:T(128)S(1)} %stack.45.me, s32[64]{0:T(128)S(1)} %copy-done.9, bf16[256,512]{1,0:T(8,128)(2,1)S(1)} %copy-done.6, bf16[256,512]{1,0:T(8,128)(2,1)S(1)} %copy-done.7, ...), custom_call_target="tpu_custom_call" | custom-call | flops 2700000000 | bytes 5000000 | tf_op jit(solution)/shard_map/pallas_call | solution.py:178
  108.9 2.5 %all-gather.1 = bf16[6,2,256,128]{3,2,1,0:T(8,128)(2,1)S(1)} all-gather(bf16[3,2,256,128]{3,2,1,0:T(8,128)(2,1)S(1)} %get-tuple-element.13), channel_id=3, replica_groups={{0,8},{16,24},{32,40},{48,56},{64,72},{80,88},{96,104},{112,120},{128,1..., dimensions={0}, use_global_device_ids=true | all-gather | bytes 1179648 | tf_op jit(solution)/shard_map/all_gather | solution.py:194
  111.5 1.9 collective-permute-start.6
  113.4 2.3 %collective-permute-start.20 = (bf16[512,768]{1,0:T(8,128)(2,1)}, bf16[512,768]{1,0:T(8,128)(2,1)}, u32[]{:S(2)}, u32[]{:S(2)}) collective-permute-start(bf16[512,768]{1,0:T(8,128)(2,1)} %collective-permute-done.19.half), channel_id=1, source_target_pairs={{0,8},{8,0},{16,24},{24,16},{32,40},{40,32},{48,56},{56,48},{64,72... | collective-permute-start | bytes 2359304 | tf_op jit(solution)/shard_map/ppermute | solution.py:225
  115.7 3.0 %collective-permute-start.8 = (bf16[2,256,128]{2,1,0:T(8,128)(2,1)S(1)}, bf16[2,256,128]{2,1,0:T(8,128)(2,1)S(1)}, u32[]{:S(2)}, u32[]{:S(2)}) collective-permute-start(bf16[2,256,128]{2,1,0:T(8,128)(2,1)S(1)} %get-tuple-element.14), channel_id=1, source_target_pairs={{8,0},{24,16},{40,32},{56,48},{72,64},{88,80},{104,96},{120,112},{... | collective-permute-start | bytes 393224 | tf_op jit(solution)/shard_map/ppermute | solution.py:244
  118.8 12.4 %collective-permute-done.6 = bf16[2,2,256,128]{3,2,1,0:T(8,128)(2,1)S(1)} collective-permute-done((bf16[2,2,256,128]{3,2,1,0:T(8,128)(2,1)S(1)}, bf16[2,2,256,128]{3,2,1,0:T(8,128)(2,1)S(1)}, u32[]{:S(2)}, u32[]{:S(2)}) %collective-permute-start.6) | collective-permute-done | bytes 262176 | tf_op jit(solution)/shard_map/ppermute | solution.py:243
  131.2 1.9 collective-permute-start.7
  133.1 3.8 %collective-permute-start.5 = (bf16[256,512]{1,0:T(8,128)(2,1)S(1)}, bf16[256,512]{1,0:T(8,128)(2,1)S(1)}, u32[]{:S(2)}, u32[]{:S(2)}) collective-permute-start(bf16[256,512]{1,0:T(8,128)(2,1)S(1)} %get-tuple-element.11.d0), channel_id=1, source_target_pairs={{0,2},{1,3},{2,4},{3,5},{4,6},{5,7},{6,0},{7,1},{8,10},{9,11},{10,... | collective-permute-start | bytes 786440 | tf_op jit(solution)/shard_map/ppermute | solution.py:251
  136.9 7.3 %collective-permute-start.4 = (bf16[256,512]{1,0:T(8,128)(2,1)S(1)}, bf16[256,512]{1,0:T(8,128)(2,1)S(1)}, u32[]{:S(2)}, u32[]{:S(2)}) collective-permute-start(bf16[256,512]{1,0:T(8,128)(2,1)S(1)} %get-tuple-element.11.d0), channel_id=1, source_target_pairs={{0,4},{1,5},{2,6},{3,7},{4,0},{5,1},{6,2},{7,3},{8,12},{9,13},{10,... | collective-permute-start | bytes 786440 | tf_op jit(solution)/shard_map/ppermute | solution.py:251
  144.3 2.4 %collective-permute-start.3 = (bf16[256,512]{1,0:T(8,128)(2,1)S(1)}, bf16[256,512]{1,0:T(8,128)(2,1)S(1)}, u32[]{:S(2)}, u32[]{:S(2)}) collective-permute-start(bf16[256,512]{1,0:T(8,128)(2,1)S(1)} %get-tuple-element.11.d0), channel_id=1, source_target_pairs={{0,6},{1,7},{2,0},{3,1},{4,2},{5,3},{6,4},{7,5},{8,14},{9,15},{10,... | collective-permute-start | bytes 786440 | tf_op jit(solution)/shard_map/ppermute | solution.py:251
  146.8 3.3 %collective-permute-done.5.d3 = bf16[256,512]{1,0:T(8,128)(2,1)S(1)} collective-permute-done((bf16[256,512]{1,0:T(8,128)(2,1)S(1)}, bf16[256,512]{1,0:T(8,128)(2,1)S(1)}, u32[]{:S(2)}, u32[]{:S(2)}) %collective-permute-start.5) | collective-permute-done | bytes 262176 | tf_op jit(solution)/shard_map/ppermute | solution.py:251
  150.0 2.3 %collective-permute-start.11 = (bf16[2,256,128]{2,1,0:T(8,128)(2,1)S(1)}, bf16[2,256,128]{2,1,0:T(8,128)(2,1)}, u32[]{:S(2)}, u32[]{:S(2)}) collective-permute-start(bf16[2,256,128]{2,1,0:T(8,128)(2,1)S(1)} %fusion.4.k0), channel_id=1, source_target_pairs={{0,2},{1,3},{2,4},{3,5},{4,6},{5,7},{6,0},{7,1},{8,10},{9,11},{10,... | collective-permute-start | bytes 393224 | tf_op jit(solution)/shard_map/ppermute | solution.py:252
  152.4 15.0 %collective-permute-done.4.d2 = bf16[256,512]{1,0:T(8,128)(2,1)S(1)} collective-permute-done((bf16[256,512]{1,0:T(8,128)(2,1)S(1)}, bf16[256,512]{1,0:T(8,128)(2,1)S(1)}, u32[]{:S(2)}, u32[]{:S(2)}) %collective-permute-start.4) | collective-permute-done | bytes 262176 | tf_op jit(solution)/shard_map/ppermute | solution.py:251
  167.4 0.7 copy-done.2
  168.1 1.9 collective-permute-start.10
  170.0 0.7 copy-done.4
  170.7 1.9 collective-permute-start.9
  172.7 6.4 %collective-permute-done.10.k2 = bf16[2,256,128]{2,1,0:T(8,128)(2,1)} collective-permute-done((bf16[2,256,128]{2,1,0:T(8,128)(2,1)S(1)}, bf16[2,256,128]{2,1,0:T(8,128)(2,1)}, u32[]{:S(2)}, u32[]{:S(2)}) %collective-permute-start.10) | collective-permute-done | bytes 131104 | tf_op jit(solution)/shard_map/ppermute | solution.py:252
  179.0 3.9 %collective-permute-done.9.k1 = bf16[2,256,128]{2,1,0:T(8,128)(2,1)} collective-permute-done((bf16[2,256,128]{2,1,0:T(8,128)(2,1)S(1)}, bf16[2,256,128]{2,1,0:T(8,128)(2,1)}, u32[]{:S(2)}, u32[]{:S(2)}) %collective-permute-start.9) | collective-permute-done | bytes 131104 | tf_op jit(solution)/shard_map/ppermute | solution.py:252
  183.0 0.9 copy-done.1
  183.9 0.9 copy-done.3
  184.9 0.9 copy-done.5
  185.8 4.3 %shard_map.74 = (bf16[256,512]{1,0:T(8,128)(2,1)S(1)}, f32[256,512]{1,0:T(8,128)S(1)}) custom-call(s32[6]{0:T(128)S(1)} %stack.45.me, bf16[256,512]{1,0:T(8,128)(2,1)S(1)} %copy-done.1, bf16[256,512]{1,0:T(8,128)(2,1)S(1)} %copy-done.5, bf16[256,512]{1,0:T(8,128)(2,1)S(1)} %copy-done.3, bf16[256,512]{1,0:T(8,128)(2,1)S(1)} %collective-permute-done.5.d3, ...), custom_call_target="tpu_custom_call" | custom-call | flops 1610612736 | bytes 8000000 | tf_op jit(solution)/shard_map/pallas_call | solution.py:178
  190.1 8.6 %all-gather.2 = bf16[512,512]{1,0:T(8,128)(2,1)S(1)} all-gather(bf16[256,512]{1,0:T(8,128)(2,1)S(1)} %get-tuple-element.16), channel_id=4, replica_groups={{0,1},{2,3},{4,5},{6,7},{8,9},{10,11},{12,13},{14,15},{16,17},{18,19},{..., dimensions={0}, use_global_device_ids=true | all-gather | bytes 786432 | tf_op jit(solution)/shard_map/all_gather | solution.py:194
  198.7 0.8 fusion
  (44 shorter events, 0.5 us)
Async XLA Ops:
  0.0 13.1 %collective-permute-start.12 = (bf16[64,768]{1,0:T(8,128)(2,1)}, bf16[64,768]{1,0:T(8,128)(2,1)S(1)}, u32[]{:S(2)}, u32[]{:S(2)}) collective-permute-start(bf16[64,768]{1,0:T(8,128)(2,1)} %bitcast.49), channel_id=1, source_target_pairs={{0,0},{1,1},{2,128},{3,129},{4,256},{5,257},{6,384},{7,385},{8,8},... | collective-permute-start | bytes 294920 | tf_op jit(solution)/shard_map/ppermute | solution.py:218
  13.1 14.6 %collective-permute-start.13 = (bf16[64,768]{1,0:T(8,128)(2,1)S(1)}, bf16[64,768]{1,0:T(8,128)(2,1)S(1)}, u32[]{:S(2)}, u32[]{:S(2)}) collective-permute-start(bf16[64,768]{1,0:T(8,128)(2,1)S(1)} %collective-permute-done.12), channel_id=1, source_target_pairs={{0,96},{8,104},{16,112},{24,120},{32,0},{40,8},{48,16},{56,24},{64... | collective-permute-start | bytes 294920 | tf_op jit(solution)/shard_map/ppermute | solution.py:220
  27.7 11.6 %collective-permute-start.14 = (bf16[128,768]{1,0:T(8,128)(2,1)S(1)}, bf16[128,768]{1,0:T(8,128)(2,1)S(1)}, u32[]{:S(2)}, u32[]{:S(2)}) collective-permute-start(bf16[128,768]{1,0:T(8,128)(2,1)S(1)} %pad_maximum_fusion.5), channel_id=1, source_target_pairs={{0,64},{8,72},{16,80},{24,88},{32,96},{40,104},{48,112},{56,120},{... | collective-permute-start | bytes 589832 | tf_op jit(solution)/shard_map/ppermute | solution.py:220
  39.4 13.7 %collective-permute-start.15 = (bf16[256,768]{1,0:T(8,128)(2,1)S(1)}, bf16[256,768]{1,0:T(8,128)(2,1)S(1)}, u32[]{:S(2)}, u32[]{:S(2)}) collective-permute-start(bf16[256,768]{1,0:T(8,128)(2,1)S(1)} %pad_maximum_fusion.3), channel_id=1, source_target_pairs={{0,16},{8,24},{16,32},{24,40},{32,48},{40,56},{48,64},{56,72},{64,... | collective-permute-start | bytes 1179656 | tf_op jit(solution)/shard_map/ppermute | solution.py:220
  53.3 6.4 %copy-start.10 = (bf16[256,128]{1,0:T(8,128)(2,1)S(1)}, bf16[256,128]{1,0:T(8,128)(2,1)}, u32[]{:S(2)}) copy-start(bf16[256,128]{1,0:T(8,128)(2,1)} %param.9) | copy-start | bytes 196612
  53.3 6.4 %copy-start.11 = (bf16[256,128]{1,0:T(8,128)(2,1)S(1)}, bf16[256,128]{1,0:T(8,128)(2,1)}, u32[]{:S(2)}) copy-start(bf16[256,128]{1,0:T(8,128)(2,1)} %param.8) | copy-start | bytes 196612
  53.3 4.3 %collective-permute-start.16 = (bf16[512,768]{1,0:T(8,128)(2,1)S(1)}, bf16[512,768]{1,0:T(8,128)(2,1)S(1)}, u32[]{:S(2)}, u32[]{:S(2)}) collective-permute-start(bf16[512,768]{1,0:T(8,128)(2,1)S(1)} %slice_dynamic-update-slice_fusion), channel_id=1, source_target_pairs={{0,8},{8,0},{16,24},{24,16},{32,40},{40,32},{48,56},{56,48},{64,72... | collective-permute-start | bytes 2359304 | tf_op jit(solution)/shard_map/ppermute | solution.py:222
  57.7 34.7 %collective-permute-start.17 = (bf16[1024,768]{1,0:T(8,128)(2,1)S(1)}, bf16[1024,768]{1,0:T(8,128)(2,1)S(1)}, u32[]{:S(2)}, u32[]{:S(2)}) collective-permute-start(bf16[1024,768]{1,0:T(8,128)(2,1)S(1)} %pad_maximum_fusion.own), channel_id=1, source_target_pairs={{0,128},{8,392},{16,144},{24,408},{32,160},{40,424},{48,176},{56,4... | collective-permute-start | bytes 4718600 | tf_op jit(solution)/shard_map/ppermute | solution.py:223
  60.4 10.3 %collective-permute-start.1 = (bf16[2,256,128]{2,1,0:T(8,128)(2,1)}, bf16[2,256,128]{2,1,0:T(8,128)(2,1)S(1)}, u32[]{:S(2)}, u32[]{:S(2)}) collective-permute-start(bf16[2,256,128]{2,1,0:T(8,128)(2,1)} %get-tuple-element.18.own), channel_id=1, source_target_pairs={{0,16},{8,24},{16,32},{24,40},{32,48},{40,56},{48,64},{56,72},{64,... | collective-permute-start | bytes 393224 | tf_op jit(solution)/shard_map/ppermute | solution.py:213
  71.4 18.5 %collective-permute-start.2 = (bf16[2,2,256,128]{3,2,1,0:T(8,128)(2,1)}, bf16[2,2,256,128]{3,2,1,0:T(8,128)(2,1)S(1)}, u32[]{:S(2)}, u32[]{:S(2)}) collective-permute-start(bf16[2,2,256,128]{3,2,1,0:T(8,128)(2,1)} %pad_maximum_fusion.4), channel_id=1, source_target_pairs={{0,32},{8,40},{16,48},{24,56},{32,64},{40,72},{48,80},{56,88},{64,... | collective-permute-start | bytes 786440 | tf_op jit(solution)/shard_map/ppermute | solution.py:215
  73.7 26.2 %collective-permute-start = (bf16[2,256,128]{2,1,0:T(8,128)(2,1)}, bf16[2,256,128]{2,1,0:T(8,128)(2,1)}, u32[]{:S(2)}, u32[]{:S(2)}) collective-permute-start(bf16[2,256,128]{2,1,0:T(8,128)(2,1)} %get-tuple-element.18.own), channel_id=1, source_target_pairs={{0,8},{16,24},{32,40},{48,56},{64,72},{80,88},{96,104},{112,120},{... | collective-permute-start | bytes 393224 | tf_op jit(solution)/shard_map/ppermute | solution.py:214
  89.9 10.0 %copy-start.6 = (bf16[256,512]{1,0:T(8,128)(2,1)S(1)}, bf16[256,512]{1,0:T(8,128)(2,1)}, u32[]{:S(2)}) copy-start(bf16[256,512]{1,0:T(8,128)(2,1)} %q_ref.1) | copy-start | bytes 786436
  89.9 10.0 %copy-start.7 = (bf16[256,512]{1,0:T(8,128)(2,1)S(1)}, bf16[256,512]{1,0:T(8,128)(2,1)}, u32[]{:S(2)}) copy-start(bf16[256,512]{1,0:T(8,128)(2,1)} %do_ref.1) | copy-start | bytes 786436
  89.9 10.0 %copy-start.8 = (bf16[256,512]{1,0:T(8,128)(2,1)S(1)}, bf16[256,512]{1,0:T(8,128)(2,1)}, u32[]{:S(2)}) copy-start(bf16[256,512]{1,0:T(8,128)(2,1)} %out_ref.1) | copy-start | bytes 786436
  89.9 10.0 %copy-start.9 = (s32[64]{0:T(128)S(1)}, s32[64]{0:T(128)}, u32[]{:S(2)}) copy-start(s32[64]{0:T(128)} %lengths.1) | copy-start | bytes 772
  92.5 20.9 %collective-permute-start.19 = (bf16[512,768]{1,0:T(8,128)(2,1)S(1)}, bf16[512,768]{1,0:T(8,128)(2,1)}, u32[]{:S(2)}, u32[]{:S(2)}) collective-permute-start(bf16[512,768]{1,0:T(8,128)(2,1)S(1)} %slice.66), channel_id=1, source_target_pairs={{0,128},{8,392},{16,144},{24,408},{32,160},{40,424},{48,176},{56,4... | collective-permute-start | bytes 2359304 | tf_op jit(solution)/shard_map/ppermute | solution.py:224
  98.0 85.0 %collective-permute-start.18 = (bf16[1024,768]{1,0:T(8,128)(2,1)S(1)}, bf16[1024,768]{1,0:T(8,128)(2,1)}, u32[]{:S(2)}, u32[]{:S(2)}) collective-permute-start(bf16[1024,768]{1,0:T(8,128)(2,1)S(1)} %collective-permute-done.17.near), channel_id=1, source_target_pairs={{0,8},{8,0},{16,24},{24,16},{32,40},{40,32},{48,56},{56,48},{64,72... | collective-permute-start | bytes 4718600 | tf_op jit(solution)/shard_map/ppermute | solution.py:225
  108.9 37.8 %copy-start = (bf16[256,512]{1,0:T(8,128)(2,1)}, bf16[256,512]{1,0:T(8,128)(2,1)S(1)}, u32[]{:S(2)}) copy-start(bf16[256,512]{1,0:T(8,128)(2,1)S(1)} %get-tuple-element.11.d0) | copy-start | bytes 786436
  111.5 19.7 %collective-permute-start.6 = (bf16[2,2,256,128]{3,2,1,0:T(8,128)(2,1)S(1)}, bf16[2,2,256,128]{3,2,1,0:T(8,128)(2,1)S(1)}, u32[]{:S(2)}, u32[]{:S(2)}) collective-permute-start(bf16[2,2,256,128]{3,2,1,0:T(8,128)(2,1)S(1)} %fusion.1), channel_id=1, source_target_pairs={{0,480},{8,488},{16,496},{24,504},{32,0},{40,8},{48,16},{56,24},{6... | collective-permute-start | bytes 786440 | tf_op jit(solution)/shard_map/ppermute | solution.py:243
  113.4 69.5 %collective-permute-start.20 = (bf16[512,768]{1,0:T(8,128)(2,1)}, bf16[512,768]{1,0:T(8,128)(2,1)}, u32[]{:S(2)}, u32[]{:S(2)}) collective-permute-start(bf16[512,768]{1,0:T(8,128)(2,1)} %collective-permute-done.19.half), channel_id=1, source_target_pairs={{0,8},{8,0},{16,24},{24,16},{32,40},{40,32},{48,56},{56,48},{64,72... | collective-permute-start | bytes 2359304 | tf_op jit(solution)/shard_map/ppermute | solution.py:225
  115.7 21.2 %collective-permute-start.8 = (bf16[2,256,128]{2,1,0:T(8,128)(2,1)S(1)}, bf16[2,256,128]{2,1,0:T(8,128)(2,1)S(1)}, u32[]{:S(2)}, u32[]{:S(2)}) collective-permute-start(bf16[2,256,128]{2,1,0:T(8,128)(2,1)S(1)} %get-tuple-element.14), channel_id=1, source_target_pairs={{8,0},{24,16},{40,32},{56,48},{72,64},{88,80},{104,96},{120,112},{... | collective-permute-start | bytes 393224 | tf_op jit(solution)/shard_map/ppermute | solution.py:244
  131.2 13.0 %collective-permute-start.7 = (bf16[2,256,128]{2,1,0:T(8,128)(2,1)S(1)}, bf16[2,256,128]{2,1,0:T(8,128)(2,1)S(1)}, u32[]{:S(2)}, u32[]{:S(2)}) collective-permute-start(bf16[2,256,128]{2,1,0:T(8,128)(2,1)S(1)} %fusion.2), channel_id=1, source_target_pairs={{0,496},{8,504},{16,0},{24,8},{32,16},{40,24},{48,32},{56,40},{64,... | collective-permute-start | bytes 393224 | tf_op jit(solution)/shard_map/ppermute | solution.py:246
  133.1 16.9 %collective-permute-start.5 = (bf16[256,512]{1,0:T(8,128)(2,1)S(1)}, bf16[256,512]{1,0:T(8,128)(2,1)S(1)}, u32[]{:S(2)}, u32[]{:S(2)}) collective-permute-start(bf16[256,512]{1,0:T(8,128)(2,1)S(1)} %get-tuple-element.11.d0), channel_id=1, source_target_pairs={{0,2},{1,3},{2,4},{3,5},{4,6},{5,7},{6,0},{7,1},{8,10},{9,11},{10,... | collective-permute-start | bytes 786440 | tf_op jit(solution)/shard_map/ppermute | solution.py:251
  136.9 30.4 %collective-permute-start.4 = (bf16[256,512]{1,0:T(8,128)(2,1)S(1)}, bf16[256,512]{1,0:T(8,128)(2,1)S(1)}, u32[]{:S(2)}, u32[]{:S(2)}) collective-permute-start(bf16[256,512]{1,0:T(8,128)(2,1)S(1)} %get-tuple-element.11.d0), channel_id=1, source_target_pairs={{0,4},{1,5},{2,6},{3,7},{4,0},{5,1},{6,2},{7,3},{8,12},{9,13},{10,... | collective-permute-start | bytes 786440 | tf_op jit(solution)/shard_map/ppermute | solution.py:251
  144.3 25.7 %collective-permute-start.3 = (bf16[256,512]{1,0:T(8,128)(2,1)S(1)}, bf16[256,512]{1,0:T(8,128)(2,1)S(1)}, u32[]{:S(2)}, u32[]{:S(2)}) collective-permute-start(bf16[256,512]{1,0:T(8,128)(2,1)S(1)} %get-tuple-element.11.d0), channel_id=1, source_target_pairs={{0,6},{1,7},{2,0},{3,1},{4,2},{5,3},{6,4},{7,5},{8,14},{9,15},{10,... | collective-permute-start | bytes 786440 | tf_op jit(solution)/shard_map/ppermute | solution.py:251
  150.0 22.6 %collective-permute-start.11 = (bf16[2,256,128]{2,1,0:T(8,128)(2,1)S(1)}, bf16[2,256,128]{2,1,0:T(8,128)(2,1)}, u32[]{:S(2)}, u32[]{:S(2)}) collective-permute-start(bf16[2,256,128]{2,1,0:T(8,128)(2,1)S(1)} %fusion.4.k0), channel_id=1, source_target_pairs={{0,2},{1,3},{2,4},{3,5},{4,6},{5,7},{6,0},{7,1},{8,10},{9,11},{10,... | collective-permute-start | bytes 393224 | tf_op jit(solution)/shard_map/ppermute | solution.py:252
  167.4 0.7 copy-start.2
  168.1 10.9 %collective-permute-start.10 = (bf16[2,256,128]{2,1,0:T(8,128)(2,1)S(1)}, bf16[2,256,128]{2,1,0:T(8,128)(2,1)}, u32[]{:S(2)}, u32[]{:S(2)}) collective-permute-start(bf16[2,256,128]{2,1,0:T(8,128)(2,1)S(1)} %fusion.4.k0), channel_id=1, source_target_pairs={{0,4},{1,5},{2,6},{3,7},{4,0},{5,1},{6,2},{7,3},{8,12},{9,13},{10,... | collective-permute-start | bytes 393224 | tf_op jit(solution)/shard_map/ppermute | solution.py:252
  170.0 0.7 copy-start.4
  170.7 12.2 %collective-permute-start.9 = (bf16[2,256,128]{2,1,0:T(8,128)(2,1)S(1)}, bf16[2,256,128]{2,1,0:T(8,128)(2,1)}, u32[]{:S(2)}, u32[]{:S(2)}) collective-permute-start(bf16[2,256,128]{2,1,0:T(8,128)(2,1)S(1)} %fusion.4.k0), channel_id=1, source_target_pairs={{0,6},{1,7},{2,0},{3,1},{4,2},{5,3},{6,4},{7,5},{8,14},{9,15},{10,... | collective-permute-start | bytes 393224 | tf_op jit(solution)/shard_map/ppermute | solution.py:252
  183.0 1.0 copy-start.1
  183.9 0.9 copy-start.3
  184.9 0.9 copy-start.5
